TPU v7x, 1024 devices: a whole 4x8x16 slice. The times are simulated.
1024 devices in a mesh: circ: 64 (over x_lo, z, core), span: 16 (over x_hi, y).
Axes of the slice: x: 4 (x_hi: 2, x_lo: 2; x = x_hi * 2 + x_lo), y: 8, z: 16, core: 2. Of those that a mesh axis runs over, the one named last changes fastest.
Arguments:
- adjoint_rotor: float32 [6, 32, 4, 16384], P(None, 'span', None, 'circ'), may hold values from -6 to 6
- adjoint_stator: float32 [6, 32, 4, 16384], P(None, 'span', None, 'circ'), may hold values from -6 to 6
- jac_diag_rotor: float32 [6, 32, 4, 16384], P(None, 'span', None, 'circ'), may hold values from 2 to 4
- jac_diag_stator: float32 [6, 32, 4, 16384], P(None, 'span', None, 'circ'), may hold values from 2 to 4
- jac_off_rotor: bfloat16 [6, 6, 32, 4, 16384], P(None, None, 'span', None, 'circ'), may hold values from -1 to 1
- jac_off_stator: bfloat16 [6, 6, 32, 4, 16384], P(None, None, 'span', None, 'circ'), may hold values from -1 to 1
- source_rotor: float32 [6, 32, 4, 16384], P(None, 'span', None, 'circ'), may hold values from -6 to 6
- source_stator: float32 [6, 32, 4, 16384], P(None, 'span', None, 'circ'), may hold values from -6 to 6
- rotor_state: bfloat16 [6, 32, 16384], P(None, 'span', 'circ'), may hold values from -6 to 6
- margin_block: int32 [32, 128, 4], P('span'), may hold values from 0 to 127, as said below
- face_count: int32 [32, 128], P('span'), may hold values from 1 to 4
- margin_weight: float32 [32, 128, 4, 128], P('span'), may hold values from 0.2 to 1
Outputs:
- rotor_adjoint: float32 [6, 32, 4, 16384], P(None, 'span', None, 'circ')
- stator_adjoint: float32 [6, 32, 4, 16384], P(None, 'span', None, 'circ')
Inputs may be any that keep to these rules, and one draw needn't show every extreme that they name: `margin_block`: entry k of the list of stator block b in spanwise row s is rotor block (b + o + 2 * 2 * s + 1 + j + k) mod 128, with one o for the whole array and j from 0 to 2 for each block of each row.
All inputs are finite; a program needn't handle non-finite values.
Results may differ from a plain program's by a relative error of at most 0.00055.
Values may be sent and summed in bfloat16 or wider, within the bound.
A program may use at most 32 MiB of HBM per device.

v0:
```python
import jax
import jax.numpy as jnp
from jax import lax
from jax.sharding import PartitionSpec as P

STEPS = 2


step_size = 0.1
coupling = 0.2
highest = lax.Precision.HIGHEST


def extended(x, sides, width):
    for axis, dim in sides:
        size, length = (lax.axis_size(axis), x.shape[dim])
        up = [(i, (i + 1) % size) for i in range(size)]
        down = [(j, i) for i, j in up]
        last = lax.slice_in_dim(x, length - width, length, axis=dim)
        first = lax.slice_in_dim(x, 0, width, axis=dim)
        before = lax.ppermute(last, axis, up)
        after = lax.ppermute(first, axis, down)
        x = jnp.concatenate([before, x, after], axis=dim)
    return x


def interface_flux(primal, adjoint):
    speeds = jnp.sqrt(1.0 + primal * primal)
    projection = jnp.sum(primal * adjoint, axis=0) / (6.0 + jnp.sum(primal * primal, axis=0))
    return speeds * adjoint + 0.5 * primal * projection[None]


def jacobian_apply(jac_diag, jac_off, adjoint):
    applied = jac_diag * adjoint
    for source_var in range(adjoint.shape[0]):
        applied = applied + jac_off[source_var].astype(jnp.float32) * adjoint[source_var][None]
    return applied


def per_device(
    adjoint_rotor,
    adjoint_stator,
    jac_diag_rotor,
    jac_diag_stator,
    jac_off_rotor,
    jac_off_stator,
    source_rotor,
    source_stator,
    rotor_state,
    margin_block,
    face_count,
    margin_weight,
):
    var_count = adjoint_rotor.shape[0]
    span_rows = adjoint_rotor.shape[1]
    layer_count = adjoint_rotor.shape[2]
    cell_count = adjoint_rotor.shape[3]
    entry_total = margin_weight.shape[2]
    block_width = margin_weight.shape[3]
    own_blocks = cell_count // block_width
    circ_at = lax.axis_index("circ")
    first_block = circ_at * own_blocks
    span_at = lax.axis_index("span")
    span_total = lax.axis_size("span")
    live_mask = (
        jnp.arange(entry_total, dtype=jnp.int32)[None, None, :] < face_count[:, :, None]
    ).astype(jnp.float32)
    weights_live = margin_weight * live_mask[:, :, :, None]
    own_ids = lax.dynamic_slice_in_dim(margin_block, first_block, own_blocks, 1)
    own_weights = lax.dynamic_slice_in_dim(weights_live, first_block, own_blocks, 1)
    portion = lax.all_gather(rotor_state, "circ", axis=2, tiled=True)
    row_count = portion.shape[2] // block_width
    blocks = portion.reshape(var_count, span_rows, row_count, block_width).astype(jnp.float32)
    pick_one_hot = (
        own_ids[:, :, :, None] == jnp.arange(row_count, dtype=jnp.int32)[None, None, None, :]
    ).astype(jnp.float32)
    pick_mixing = jnp.einsum("sbkj,sbkc->sbjc", pick_one_hot, own_weights, precision=highest)
    stator_primal = jnp.einsum("sbjc,vsjc->vsbc", pick_mixing, blocks, precision=highest).reshape(
        var_count, span_rows, cell_count
    )
    low_keep = jnp.where(span_at == 0, 0.0, 1.0).astype(jnp.float32)
    high_keep = jnp.where(span_at == span_total - 1, 0.0, 1.0).astype(jnp.float32)
    below_mask = jnp.ones((span_rows,), jnp.float32).at[0].set(low_keep)[None, None, :, None, None]
    above_mask = (
        jnp.ones((span_rows,), jnp.float32)
        .at[span_rows - 1]
        .set(high_keep)[None, None, :, None, None]
    )
    rotor_adj, stator_adj = (adjoint_rotor, adjoint_stator)
    for sweep in range(STEPS):
        stacked = jnp.stack((rotor_adj, stator_adj))
        padded = extended(stacked.astype(jnp.bfloat16), (("circ", 4), ("span", 2)), 1).astype(
            stacked.dtype
        )
        inner = padded[:, :, 1:-1, :, :]
        beside_all = inner[:, :, :, :, 2:] + inner[:, :, :, :, :-2]
        layer_pad = jnp.pad(stacked, ((0, 0), (0, 0), (0, 0), (1, 1), (0, 0)))
        beside_all = beside_all + layer_pad[:, :, :, 2:] + layer_pad[:, :, :, :-2]
        beside_all = (
            beside_all
            + padded[:, :, :-2, :, 1:-1] * below_mask
            + padded[:, :, 2:, :, 1:-1] * above_mask
        )
        face_flux = interface_flux(stator_primal, stator_adj[:, :, 0, :])
        flux_wire = face_flux.astype(jnp.bfloat16)
        flux_blocks = flux_wire.astype(jnp.float32).reshape(
            var_count, span_rows, own_blocks, block_width
        )
        one_hot = (
            own_ids[:, :, :, None]
            == jnp.arange(own_blocks * lax.axis_size("circ"), dtype=jnp.int32)[None, None, None, :]
        ).astype(jnp.float32)
        mixing = jnp.einsum("sbkj,sbkc->sbjc", one_hot, own_weights, precision=highest)
        pulled_blocks = lax.psum_scatter(
            jnp.einsum("sbjc,vsbc->jvsc", mixing, flux_blocks, precision=highest),
            "circ",
            scatter_dimension=0,
            tiled=True,
        )
        pulled = jnp.transpose(pulled_blocks, (1, 2, 0, 3)).reshape(
            var_count, span_rows, cell_count
        )
        rotor_res = (
            jacobian_apply(jac_diag_rotor, jac_off_rotor, rotor_adj)
            - coupling * beside_all[0]
            - source_rotor
        )
        rotor_res = rotor_res.at[:, :, layer_count - 1, :].add(-pulled)
        stator_res = (
            jacobian_apply(jac_diag_stator, jac_off_stator, stator_adj)
            - coupling * beside_all[1]
            - source_stator
        )
        stator_res = stator_res.at[:, :, 0, :].add(face_flux)
        rotor_adj = rotor_adj - step_size * rotor_res
        stator_adj = stator_adj - step_size * stator_res
    return (rotor_adj, stator_adj)


def solution(mesh):
    placed = (
        P(None, "span", None, "circ"),
        P(None, "span", None, "circ"),
        P(None, "span", None, "circ"),
        P(None, "span", None, "circ"),
        P(None, None, "span", None, "circ"),
        P(None, None, "span", None, "circ"),
        P(None, "span", None, "circ"),
        P(None, "span", None, "circ"),
        P(None, "span", "circ"),
        P("span", None, None),
        P("span", None),
        P("span", None, None, None),
    )
    return jax.shard_map(
        per_device,
        mesh=mesh,
        in_specs=placed,
        out_specs=(P(None, "span", None, "circ"), P(None, "span", None, "circ")),
        check_vma=False,
    )
```

profile of v0, /device:TPU:1, one launch (start us, length us, event | category | flops | bytes accessed | tf_op | source)
XLA Modules:
  0.0 578.0 jit_solution(7675523478203730253)
XLA Ops:
  7.2 0.9 copy_bitcast_fusion
  8.3 5.4 collective-permute-start
  13.7 12.6 %collective-permute-start.1 = (bf16[2,6,2,4,1]{4,2,1,3,0:T(2,128)(2,1)S(1)}, bf16[2,6,2,4,1]{4,2,1,3,0:T(2,128)(2,1)S(1)}, u32[]{:S(2)}, u32[]{:S(2)}) collective-permute-start(bf16[2,6,2,4,1]{4,2,1,3,0:T(2,128)(2,1)S(1)} %get-tuple-element.129), channel_id=1, source_target_pairs={{16,0},{32,16},{48,32},{64,48},{80,64},{96,80},{112,96},{128,112},... | collective-permute-start | bytes 584 | tf_op jit(solution)/shard_map/ppermute | solution.py:22
  27.4 1.2 fusion.51
  29.2 66.4 %all_gather.3 = bf16[6,2,16384]{2,1,0:T(2,128)(2,1)S(1)} all-gather(bf16[6,2,256]{2,1,0:T(2,128)(2,1)S(1)} %copy-done.9), channel_id=1, replica_groups=mesh['circ'=64,'span'=16] {'circ'}, dimensions={2}, use_global_device_ids=true | all-gather | bytes 399360 | tf_op jit(solution)/shard_map/all_gather | solution.py:71
  96.3 1.0 fusion.63
  97.6 3.2 collective-permute-start.2
  100.8 6.0 %collective-permute-start.3 = (bf16[2,6,1,4,258]{4,2,1,3,0:T(2,128)(2,1)S(1)}, bf16[2,6,1,4,258]{4,2,1,3,0:T(2,128)(2,1)S(1)}, u32[]{:S(2)}, u32[]{:S(2)}) collective-permute-start(bf16[2,6,1,4,258]{4,2,1,3,0:T(2,128)(2,1)S(1)} %get-tuple-element.99), channel_id=1, source_target_pairs={{1,0},{2,1},{3,2},{4,3},{5,4},{6,5},{7,6},{8,7},{9,8},{10,9},{11,1... | collective-permute-start | bytes 74312 | tf_op jit(solution)/shard_map/ppermute | solution.py:22
  107.4 0.8 collective-permute-done.3
  110.0 1.1 convolution_bitcast_fusion
  111.1 1.2 copy.183
  112.5 1.1 convolution_bitcast_fusion.1
  113.7 1.2 copy.158
  114.9 0.8 copy-done.1
  115.8 1.3 dynamic-slice.44
  117.8 0.8 copy-done.3
  118.8 430.2 %all-reduce.9.cloned.1.call-done = (f32[128,6,2,128]{3,2,1,0:T(2,128)}, f32[128,6,2,128]{3,2,1,0:T(2,128)}) async-done(((f32[128,6,2,128]{3,2,1,0:T(2,128)}, f32[128,6,2,128]{3,2,1,0:T(2,128)}), (f32[128,6,2,128]{3,2,1,0:T(2,128)}, f32[128,6,2,128]{3,2,1,0:T(2,128)})) %all-reduce.9.cloned.1.call-update) | async-done | bytes 1572880
  549.0 0.7 fusion.50
  550.0 2.9 collective-permute-start.4
  552.9 1.9 collective-permute-start.5
  554.9 3.2 collective-permute-done.5
  558.4 3.1 collective-permute-start.6
  561.5 5.8 %collective-permute-start.7 = (bf16[2,6,1,4,258]{4,2,1,3,0:T(2,128)(2,1)S(1)}, bf16[2,6,1,4,258]{4,2,1,3,0:T(2,128)(2,1)S(1)}, u32[]{:S(2)}, u32[]{:S(2)}) collective-permute-start(bf16[2,6,1,4,258]{4,2,1,3,0:T(2,128)(2,1)S(1)} %get-tuple-element.97), channel_id=1, source_target_pairs={{1,0},{2,1},{3,2},{4,3},{5,4},{6,5},{7,6},{8,7},{9,8},{10,9},{11,1... | collective-permute-start | bytes 74312 | tf_op jit(solution)/shard_map/ppermute | solution.py:22
  567.3 0.7 fusion.49
  (102 shorter events, 9.4 us)
Async XLA Ops:
  7.2 20.0 %copy-start = (s32[2,128,4]{1,2,0:T(4,128)S(1)}, s32[2,128,4]{1,2,0:T(4,128)}, u32[]{:S(2)}) copy-start(s32[2,128,4]{1,2,0:T(4,128)} %param.33) | copy-start | bytes 12292
  7.2 541.8 %all-reduce.9.cloned.1.call-start = ((), (), s32[]{:S(2)}) async-start(), calls=%async_computation | async-start | bytes 3145728
  8.1 18.2 %copy-start.7 = (bf16[6,6,2,4,256]{4,3,2,1,0:T(4,128)(2,1)S(1)}, bf16[6,6,2,4,256]{4,3,2,1,0:T(4,128)(2,1)}, u32[]{:S(2)}) copy-start(bf16[6,6,2,4,256]{4,3,2,1,0:T(4,128)(2,1)} %param.29) | copy-start | bytes 442372
  8.3 89.0 %collective-permute-start = (bf16[2,6,2,4,1]{4,2,1,3,0:T(2,128)(2,1)S(1)}, bf16[2,6,2,4,1]{4,2,1,3,0:T(2,128)(2,1)S(1)}, u32[]{:S(2)}, u32[]{:S(2)}) collective-permute-start(bf16[2,6,2,4,1]{4,2,1,3,0:T(2,128)(2,1)S(1)} %get-tuple-element.128), channel_id=1, source_target_pairs={{0,16},{16,32},{32,48},{48,64},{64,80},{80,96},{96,112},{112,128},... | collective-permute-start | bytes 584 | tf_op jit(solution)/shard_map/ppermute | solution.py:21
  13.7 83.6 %collective-permute-start.1 = (bf16[2,6,2,4,1]{4,2,1,3,0:T(2,128)(2,1)S(1)}, bf16[2,6,2,4,1]{4,2,1,3,0:T(2,128)(2,1)S(1)}, u32[]{:S(2)}, u32[]{:S(2)}) collective-permute-start(bf16[2,6,2,4,1]{4,2,1,3,0:T(2,128)(2,1)S(1)} %get-tuple-element.129), channel_id=1, source_target_pairs={{16,0},{32,16},{48,32},{64,48},{80,64},{96,80},{112,96},{128,112},... | collective-permute-start | bytes 584 | tf_op jit(solution)/shard_map/ppermute | solution.py:22
  26.4 0.7 copy-start.10
  28.5 0.7 copy-start.9
  96.2 1.0 copy-start.2
  97.6 9.8 %collective-permute-start.2 = (bf16[2,6,1,4,258]{4,2,1,3,0:T(2,128)(2,1)S(1)}, bf16[2,6,1,4,258]{4,2,1,3,0:T(2,128)(2,1)S(1)}, u32[]{:S(2)}, u32[]{:S(2)}) collective-permute-start(bf16[2,6,1,4,258]{4,2,1,3,0:T(2,128)(2,1)S(1)} %get-tuple-element.98), channel_id=1, source_target_pairs={{0,1},{1,2},{2,3},{3,4},{4,5},{5,6},{6,7},{7,8},{8,9},{9,10},{10,1... | collective-permute-start | bytes 74312 | tf_op jit(solution)/shard_map/ppermute | solution.py:21
  100.8 7.4 %collective-permute-start.3 = (bf16[2,6,1,4,258]{4,2,1,3,0:T(2,128)(2,1)S(1)}, bf16[2,6,1,4,258]{4,2,1,3,0:T(2,128)(2,1)S(1)}, u32[]{:S(2)}, u32[]{:S(2)}) collective-permute-start(bf16[2,6,1,4,258]{4,2,1,3,0:T(2,128)(2,1)S(1)} %get-tuple-element.99), channel_id=1, source_target_pairs={{1,0},{2,1},{3,2},{4,3},{5,4},{6,5},{7,6},{8,7},{9,8},{10,9},{11,1... | collective-permute-start | bytes 74312 | tf_op jit(solution)/shard_map/ppermute | solution.py:22
  108.5 0.8 copy-start.5
  108.6 0.8 copy-start.6
  114.9 0.8 copy-start.1
  114.9 2.8 copy-start.8
  117.8 0.8 copy-start.3
  117.8 0.8 copy-start.4
  550.0 4.9 collective-permute-start.4
  552.9 5.1 collective-permute-start.5
  558.4 9.7 %collective-permute-start.6 = (bf16[2,6,1,4,258]{4,2,1,3,0:T(2,128)(2,1)S(1)}, bf16[2,6,1,4,258]{4,2,1,3,0:T(2,128)(2,1)S(1)}, u32[]{:S(2)}, u32[]{:S(2)}) collective-permute-start(bf16[2,6,1,4,258]{4,2,1,3,0:T(2,128)(2,1)S(1)} %get-tuple-element.96), channel_id=1, source_target_pairs={{0,1},{1,2},{2,3},{3,4},{4,5},{5,6},{6,7},{7,8},{8,9},{9,10},{10,1... | collective-permute-start | bytes 74312 | tf_op jit(solution)/shard_map/ppermute | solution.py:21
  561.5 7.2 %collective-permute-start.7 = (bf16[2,6,1,4,258]{4,2,1,3,0:T(2,128)(2,1)S(1)}, bf16[2,6,1,4,258]{4,2,1,3,0:T(2,128)(2,1)S(1)}, u32[]{:S(2)}, u32[]{:S(2)}) collective-permute-start(bf16[2,6,1,4,258]{4,2,1,3,0:T(2,128)(2,1)S(1)} %get-tuple-element.97), channel_id=1, source_target_pairs={{1,0},{2,1},{3,2},{4,3},{5,4},{6,5},{7,6},{8,7},{9,8},{10,9},{11,1... | collective-permute-start | bytes 74312 | tf_op jit(solution)/shard_map/ppermute | solution.py:22
Sparse Core Ops, SparseCore 0:
  115.0 433.9 all-reduce.8
where the time goes:
time: 582 us; the launch traced here: 578 us
  waiting for transfers between devices  435 us (75%)
  blocking collectives  66.4 us (11%)
  starting transfers between devices  40.9 us (7%)
  between operations  15.3 us (3%)
  local copies, waits for them, and re-layouts  11.3 us (2%)
    unnamed x2, waiting for transfers between devices  430 us
    all_gather x1, blocking collectives, per_device(): portion = lax.all_gather(rotor_state, 'circ', axis=2, tiled=True)  66.4 us
    ppermute x4, starting transfers between devices, extended(): after = lax.ppermute(first, axis, down)  26.3 us
    ppermute x4, starting transfers between devices, extended(): before = lax.ppermute(last, axis, up)  14.6 us
  transfers between devices with their start and end apart: 9, of which 5 were waited for; matrix products, arithmetic and copies ran while one was open for 1% of the time, Pallas kernels for 0%

commit v1 on v0

v1 whole, which is shorter than its diff:
```python
import functools

import jax
import jax.numpy as jnp
from jax import lax
from jax.experimental import pallas as pl
from jax.experimental.pallas import tpu as pltpu
from jax.sharding import PartitionSpec as P

STEPS = 2
STEP_SIZE = 0.1
COUPLING = 0.2
COARSE = 8
REACH = 3
LOW = COARSE // 2 + REACH
SLOTS = COARSE + 2 * REACH
HIGH = SLOTS - 1 - LOW


def kernel(
    ring,
    band,
    adj_r,
    adj_s,
    diag_r,
    diag_s,
    off_r,
    off_s,
    src_r,
    src_s,
    rstate,
    margin,
    count,
    weight,
    out_r,
    out_s,
    adj,
    diag,
    off,
    src,
    wts,
    lists,
    live,
    pick,
    pad,
    part,
    adj1,
    edge,
    rows,
    near_a,
    near_b,
    near_f,
    sent_f,
    prim,
    face,
    flux,
    far_a0,
    far_a1,
    far_b,
    far_f,
    sent_b,
    pull,
    in_sem,
    out_sem,
    edge_sem,
    near_sem,
    far_sem,
    send_sem,
):
    far_a = (far_a0, far_a1)
    c = lax.axis_index("circ")
    s = lax.axis_index("span")

    def circ(shift):
        return {"circ": lax.rem(c + (shift + ring), ring)}

    def span(shift):
        return {"span": lax.rem(s + (shift + band), band)}

    def remote(source, target, sent, landed, where):
        return pltpu.make_async_remote_copy(
            src_ref=source,
            dst_ref=target,
            send_sem=sent,
            recv_sem=landed,
            device_id=where,
            device_id_type=pl.DeviceIdType.MESH,
        )

    loads = [
        (margin, lists),
        (count, live),
        (adj_r, adj.at[0]),
        (adj_s, adj.at[1]),
        (rstate, pick),
        (off_r, off.at[0]),
        (off_s, off.at[1]),
        (diag_r, diag.at[0]),
        (diag_s, diag.at[1]),
        (src_r, src.at[0]),
        (src_s, src.at[1]),
        (weight, wts),
    ]
    copies = [pltpu.make_async_copy(a, b, in_sem.at[i]) for i, (a, b) in enumerate(loads)]
    for one in copies:
        one.start()

    barrier = pltpu.get_barrier_semaphore()

    def greet(where):
        pl.semaphore_signal(
            barrier, inc=1, device_id=where, device_id_type=pl.DeviceIdType.MESH
        )

    for shift in range(1, COARSE):
        greet(circ(shift))
        greet(circ(-shift))
    for shift in range(COARSE, ring, COARSE):
        greet(circ(shift))
    greet(span(1))
    greet(span(-1))

    def coarse(piece, landing, sign, landed, sent):
        @pl.loop(1, COARSE)
        def _(a):
            remote(piece, landing.at[a], sent, landed, circ(sign * COARSE * a)).start()

    def fine(piece, landing, sign, landed, sent):
        @pl.loop(1, HIGH + 1)
        def _(t):
            remote(piece, landing.at[t], sent, landed, circ(sign * t)).start()

        @pl.loop(1, LOW + 1)
        def _(t):
            remote(piece, landing.at[SLOTS - t], sent, landed, circ(-sign * t)).start()

    def drain(view, sem):
        pltpu.make_async_copy(view, view, sem).wait()

    def edges(source, step, first, last):
        lower = source.at[first:last, :, :, :, pl.ds(0, 128)]
        upper = source.at[first:last, :, :, :, pl.ds(128, 128)]
        sems = edge_sem.at[step, first]
        return [
            remote(upper, edge.at[step, 0, first:last], sems.at[4], sems.at[0], circ(1)),
            remote(lower, edge.at[step, 1, first:last], sems.at[5], sems.at[1], circ(-1)),
            remote(
                source.at[first:last, :, 1],
                rows.at[step, 0, first:last],
                sems.at[6],
                sems.at[2],
                span(1),
            ),
            remote(
                source.at[first:last, :, 0],
                rows.at[step, 1, first:last],
                sems.at[7],
                sems.at[3],
                span(-1),
            ),
        ]

    pad[...] = jnp.zeros_like(pad)
    copies[2].wait()
    copies[3].wait()
    pl.semaphore_wait(barrier, 2 * (COARSE - 1) + ring // COARSE - 1 + 2)

    coarse(rstate, near_a, -1, near_sem.at[0], send_sem.at[0])
    first_edges = edges(adj, 0, 0, 2)
    for one in first_edges:
        one.start()

    copies[0].wait()
    copies[1].wait()
    base = lists[0, 0, 0]
    shift = lax.shift_right_logical(base, 1) + 2
    fine_at = ((shift + COARSE // 2) & (COARSE - 1)) - COARSE // 2
    coarse_at = lax.shift_right_logical(shift - fine_at + ring, 3) & (COARSE - 1)

    copies[4].wait()
    near_a[0] = pick[...]
    drain(near_a.at[pl.ds(1, COARSE - 1)], near_sem.at[0])
    chosen = near_a[coarse_at]
    sent_f[...] = chosen
    near_b[0] = chosen
    fine(sent_f, near_b, -1, near_sem.at[1], send_sem.at[1])

    def local_part(x, field):
        pad[field, :, :, 1:5, :] = x[...]
        value = diag[field] * x[...] - src[field]
        value = value - COUPLING * (pad[field, :, :, 0:4, :] + pad[field, :, :, 2:6, :])

        def add(w, total):
            return total + off[field, w].astype(jnp.float32) * x[w][None]

        part[field] = lax.fori_loop(0, off.shape[1], add, value)

    lane = lax.broadcasted_iota(jnp.int32, (1, 1, 1, 128), 3)
    below = jnp.where(s == 0, 0.0, 1.0).astype(jnp.float32)
    above = jnp.where(s == band - 1, 0.0, 1.0).astype(jnp.float32)

    def advance(x, result, field, step):
        for half in range(2):
            here = pl.ds(half * 128, 128)
            other = pl.ds(128 - half * 128, 128)
            mine = x[:, :, :, here]
            before = edge[step, 0, field] if half == 0 else x[:, :, :, other]
            after = x[:, :, :, other] if half == 0 else edge[step, 1, field]
            left = pltpu.roll(jnp.where(lane == 127, before, mine), 1, axis=3)
            right = pltpu.roll(jnp.where(lane == 0, after, mine), 127, axis=3)
            beside = left + right
            spanwise0 = rows[step, 0, field, :, :, here] * below + x[:, 1, :, here]
            spanwise1 = rows[step, 1, field, :, :, here] * above + x[:, 0, :, here]
            whole = part[field, :, :, :, here] - COUPLING * beside
            result[:, 0, :, here] = mine[:, 0] - STEP_SIZE * (whole[:, 0] - COUPLING * spanwise0)
            result[:, 1, :, here] = mine[:, 1] - STEP_SIZE * (whole[:, 1] - COUPLING * spanwise1)

    for one in copies[5:]:
        one.wait()
    for field in (1, 0):
        local_part(adj.at[field], field)
    for one in first_edges:
        one.wait()
    for field in (1, 0):
        advance(adj.at[field], adj1.at[field], field, 0)

    drain(near_b.at[pl.ds(1, SLOTS - 1)], near_sem.at[1])
    for half in range(2):
        near_f[:, half] = near_b[:, :, :, pl.ds(half * 128, 128)].astype(jnp.float32)

    def spot(delta, sign):
        delta = (delta + 2 * REACH) & (2 * ring - 1)
        w = lax.shift_right_logical(delta, 1) - REACH
        t = fine_at + sign * w
        t = t + (SLOTS & lax.shift_right_arithmetic(t, 31))
        return jnp.minimum(t, SLOTS - 1), delta & 1

    def masked(factor, k, alive):
        shape = factor.shape
        return jnp.where(jnp.full(shape, k) < jnp.full(shape, alive), factor, 0.0)

    for row in range(2):
        for block in range(2):
            b = 2 * c + block
            head = lists[row, 0, b]
            alive = live[row, b]
            total = jnp.zeros((6, 1, 128), jnp.float32)
            for k in range(4):
                slot, half = spot(head + k - 2 * c - 2 * shift, 1)
                got = near_f[slot, half, :, row : row + 1, :]
                total = total + masked(wts[row, b, k : k + 1, :], k, alive)[None] * got
            prim[:, row : row + 1, pl.ds(block * 128, 128)] = total

    for row in range(2):
        face[:, row : row + 1, :] = adj[1, :, row, 0:1, :]
    q = prim[...]
    speeds = jnp.sqrt(1.0 + q * q)
    norm = 6.0 + jnp.sum(q * q, axis=0)

    def interface_flux(p):
        projection = jnp.sum(q * p, axis=0) / norm
        return speeds * p + 0.5 * q * projection[None]

    for step in range(STEPS):
        value = interface_flux(face[...])
        flux[...] = value
        wire = value.astype(jnp.bfloat16)
        sent_b[step, 0] = wire
        far_a[step][0] = wire
        coarse(sent_b.at[step, 0], far_a[step], 1, far_sem.at[step, 0], send_sem.at[2 + 2 * step])
        if step == 0:
            for row in range(2):
                first = adj1[1, :, row, 0:1, :] - STEP_SIZE * flux[:, row : row + 1, :]
                adj1[1, :, row, 0:1, :] = first
                face[:, row : row + 1, :] = first

    stator_edges = edges(adj1, 1, 1, 2)
    for one in stator_edges:
        one.start()

    for step in range(STEPS):
        drain(far_a[step].at[pl.ds(1, COARSE - 1)], far_sem.at[step, 0])
        chosen = far_a[step][coarse_at]
        sent_b[step, 1] = chosen
        far_b[step, 0] = chosen
        fine(sent_b.at[step, 1], far_b.at[step], 1, far_sem.at[step, 1], send_sem.at[3 + 2 * step])

    local_part(adj1.at[1], 1)
    for one in stator_edges:
        one.wait()
    advance(adj1.at[1], adj.at[1], 1, 1)
    for row in range(2):
        adj[1, :, row, 0:1, :] = adj[1, :, row, 0:1, :] - STEP_SIZE * flux[:, row : row + 1, :]
    store_s = pltpu.make_async_copy(adj.at[1], out_s, out_sem.at[0])
    store_s.start()

    def pulled(step):
        drain(far_b.at[step, pl.ds(1, SLOTS - 1)], far_sem.at[step, 1])
        for half in range(2):
            far_f[:, half] = far_b[step, :, :, :, pl.ds(half * 128, 128)].astype(jnp.float32)
        for row in range(2):
            for block in range(2):
                r = 2 * c + block
                total = jnp.zeros((6, 1, 128), jnp.float32)
                for m in range(-2, 6):
                    b = (r - base - 4 * row - m + 4 * ring) & (2 * ring - 1)
                    k = (r - lists[row, 0, b] + 2 * ring) & (2 * ring - 1)
                    slot, half = spot(b - 2 * c + 2 * shift, -1)
                    got = far_f[slot, half, :, row : row + 1, :]
                    factor = wts[row, b, pl.ds(jnp.minimum(k, 3), 1), :]
                    total = total + masked(factor, k, live[row, b])[None] * got
                pull[:, row : row + 1, pl.ds(block * 128, 128)] = total

    pulled(0)
    for row in range(2):
        adj1[0, :, row, 3:4, :] = adj1[0, :, row, 3:4, :] + STEP_SIZE * pull[:, row : row + 1, :]
    rotor_edges = edges(adj1, 1, 0, 1)
    for one in rotor_edges:
        one.start()
    local_part(adj1.at[0], 0)
    pulled(1)
    for one in rotor_edges:
        one.wait()
    advance(adj1.at[0], adj.at[0], 0, 1)
    for row in range(2):
        adj[0, :, row, 3:4, :] = adj[0, :, row, 3:4, :] + STEP_SIZE * pull[:, row : row + 1, :]
    store_r = pltpu.make_async_copy(adj.at[0], out_r, out_sem.at[1])
    store_r.start()

    drain(near_a.at[pl.ds(1, COARSE - 1)], send_sem.at[0])
    drain(near_b.at[pl.ds(1, SLOTS - 1)], send_sem.at[1])
    for step in range(STEPS):
        drain(far_a[step].at[pl.ds(1, COARSE - 1)], send_sem.at[2 + 2 * step])
        drain(far_b.at[step, pl.ds(1, SLOTS - 1)], send_sem.at[3 + 2 * step])
    store_s.wait()
    store_r.wait()


def solution(mesh):
    ring, band = mesh.shape["circ"], mesh.shape["span"]

    def per_device(
        adjoint_rotor,
        adjoint_stator,
        jac_diag_rotor,
        jac_diag_stator,
        jac_off_rotor,
        jac_off_stator,
        source_rotor,
        source_stator,
        rotor_state,
        margin_block,
        face_count,
        margin_weight,
    ):
        f32, bf16 = jnp.float32, jnp.bfloat16
        shape = adjoint_rotor.shape
        piece = rotor_state.shape
        lists = jnp.transpose(margin_block, (0, 2, 1))
        out = jax.ShapeDtypeStruct(shape, f32)
        hbm = pl.BlockSpec(memory_space=pltpu.HBM)
        return pl.pallas_call(
            functools.partial(kernel, ring, band),
            out_shape=(out, out),
            in_specs=[hbm] * 12,
            out_specs=(hbm, hbm),
            scratch_shapes=[
                pltpu.VMEM((2,) + shape, f32),
                pltpu.VMEM((2,) + shape, f32),
                pltpu.VMEM((2,) + jac_off_rotor.shape, bf16),
                pltpu.VMEM((2,) + shape, f32),
                pltpu.VMEM(margin_weight.shape, f32),
                pltpu.SMEM(lists.shape, jnp.int32),
                pltpu.SMEM(face_count.shape, jnp.int32),
                pltpu.VMEM(piece, bf16),
                pltpu.VMEM((2, 6, 2, 8, 256), f32),
                pltpu.VMEM((2,) + shape, f32),
                pltpu.VMEM((2,) + shape, f32),
                pltpu.VMEM((STEPS, 2, 2, 6, 2, 4, 128), f32),
                pltpu.VMEM((STEPS, 2, 2, 6, 4, 256), f32),
                pltpu.VMEM((COARSE,) + piece, bf16),
                pltpu.VMEM((SLOTS,) + piece, bf16),
                pltpu.VMEM((SLOTS, 2, 6, 2, 128), f32),
                pltpu.VMEM(piece, bf16),
                pltpu.VMEM(piece, f32),
                pltpu.VMEM(piece, f32),
                pltpu.VMEM(piece, f32),
                pltpu.VMEM((COARSE,) + piece, bf16),
                pltpu.VMEM((COARSE,) + piece, bf16),
                pltpu.VMEM((STEPS, SLOTS) + piece, bf16),
                pltpu.VMEM((SLOTS, 2, 6, 2, 128), f32),
                pltpu.VMEM((STEPS, 2) + piece, bf16),
                pltpu.VMEM(piece, f32),
                pltpu.SemaphoreType.DMA((12,)),
                pltpu.SemaphoreType.DMA((2,)),
                pltpu.SemaphoreType.DMA((STEPS, 2, 8)),
                pltpu.SemaphoreType.DMA((2,)),
                pltpu.SemaphoreType.DMA((STEPS, 2)),
                pltpu.SemaphoreType.DMA((6,)),
            ],
            compiler_params=pltpu.CompilerParams(
                collective_id=0, has_side_effects=True, vmem_limit_bytes=60 * 1024 * 1024
            ),
            name="sweep",
        )(
            adjoint_rotor,
            adjoint_stator,
            jac_diag_rotor,
            jac_diag_stator,
            jac_off_rotor,
            jac_off_stator,
            source_rotor,
            source_stator,
            rotor_state,
            lists,
            face_count,
            margin_weight,
        )

    field = P(None, "span", None, "circ")
    matrix = P(None, None, "span", None, "circ")
    placed = (field,) * 4 + (matrix,) * 2 + (field,) * 2
    placed = placed + (
        P(None, "span", "circ"),
        P("span", None, None),
        P("span", None),
        P("span", None, None, None),
    )
    return jax.shard_map(
        per_device, mesh=mesh, in_specs=placed, out_specs=(field, field), check_vma=False
    )
```

time: 582 us -> 59.1 us (0.10)
  waiting for transfers between devices: 435 us -> 0 us
  blocking collectives: 66.4 us -> 0 us
  Pallas kernels: 0 us -> 56.1 us
  starting transfers between devices: 40.9 us -> 0 us
  between operations: 15.3 us -> 0.65 us
  local copies, waits for them, and re-layouts: 11.3 us -> 2.06 us
    unnamed x2 -> x0, waiting for transfers between devices: 430 us -> none
    all_gather x1 -> x0, blocking collectives: 66.4 us -> none  [per_device(): portion = lax.all_gather(rotor_state, 'circ', axis=2, tiled=True)]
    pallas_call x0 -> x1, Pallas kernels: none -> 56.1 us  [per_device(): pl.pallas_call(functools.partial(kernel, ring, band), out_shape=(out, out...]
    ppermute x8 -> x0, starting transfers between devices: 40.9 us -> none  [the longest x4 26.3 us: extended(): after = lax.ppermute(first, axis, down)]
  transfers between devices with their start and end apart: 9 -> 0, of which waited for: 5 -> 0; matrix products, arithmetic and copies ran while one was open for 1% -> 0% of each run, Pallas kernels for 0% -> 0%
where the time goes in v1:
time: 59.1 us; the launch traced here: 58.9 us
  Pallas kernels  56.1 us (95%)
  local copies, waits for them, and re-layouts  2.06 us (3%)
  between operations  0.65 us (1%)
    pallas_call x1, Pallas kernels, per_device(): pl.pallas_call(functools.partial(kernel, ring, band), out_shape=(out, out...  56.1 us
    unnamed x4, local copies, waits for them, and re-layouts  2.06 us

profile of v1, /device:TPU:1, one launch (start us, length us, event | category | flops | bytes accessed | tf_op | source)
XLA Modules:
  0.0 58.9 jit_solution(18269092007674716461)
XLA Ops:
  0.6 56.1 %sweep.1 = (f32[6,2,4,256]{3,2,1,0:T(4,128)}, f32[6,2,4,256]{3,2,1,0:T(4,128)}) custom-call(f32[6,2,4,256]{3,2,1,0:T(4,128)} %adj_r.1, f32[6,2,4,256]{3,2,1,0:T(4,128)} %adj_s.1, f32[6,2,4,256]{3,2,1,0:T(4,128)} %diag_r.1, f32[6,2,4,256]{3,2,1,0:T(4,128)} %diag_s.1, bf16[6,6,2,4,256]{4,3,2,1,0:T(4,128)(2,1)} %off_r.1, bf16[6,6,2,4,256]{4,3,2,1,0:T(4,128)(2,1)} %off_s.1, ...), custom_call_target="tpu_custom_call" | custom-call | tf_op jit(solution)/shard_map/sweep/pallas_call | solution.py:362
  56.8 0.0 copy-start
  56.8 1.4 %copy.16 = f32[6,2,4,256]{3,2,1,0:T(4,128)} copy(f32[6,2,4,256]{3,2,1,0:T(4,128)} %get-tuple-element.4) | data formatting | bytes 98304
  58.2 0.0 copy-done
  58.2 0.6 %copy.17 = f32[6,2,4,256]{3,2,1,0:T(4,128)} copy(f32[6,2,4,256]{3,2,1,0:T(4,128)S(1)} %copy-done) | data formatting | bytes 98304
Async XLA Ops:
  56.8 1.4 %copy-start = (f32[6,2,4,256]{3,2,1,0:T(4,128)S(1)}, f32[6,2,4,256]{3,2,1,0:T(4,128)}, u32[]{:S(2)}) copy-start(f32[6,2,4,256]{3,2,1,0:T(4,128)} %get-tuple-element.5) | copy-start | bytes 147460

commit v2 on v1

v2 whole, which is shorter than its diff:
```python
import functools

import jax
import jax.numpy as jnp
from jax import lax
from jax.experimental import pallas as pl
from jax.experimental.pallas import tpu as pltpu
from jax.sharding import PartitionSpec as P

STEPS = 2
STEP_SIZE = 0.1
COUPLING = 0.2
COARSE = 8
STRIDE = 8
OFFSET = 4
REACH = 6
SLOTS = 2 * REACH + 1
BESIDE = 3
HOMES = 2 * BESIDE + 1
SEEN = 7


def kernel(
    ring,
    band,
    adj_r,
    adj_s,
    diag_r,
    diag_s,
    off_r,
    off_s,
    src_r,
    src_s,
    rstate,
    margin,
    count,
    weight,
    out_r,
    out_s,
    adj,
    diag,
    off,
    src,
    wts,
    lists,
    live,
    pick,
    pad,
    part,
    adj1,
    edge,
    rows,
    home,
    home_f,
    near_a,
    near_b,
    near_f,
    sent_n,
    prim,
    face,
    flux,
    far_a0,
    far_a1,
    far_b0,
    far_b1,
    sent_f,
    qtab,
    ptab,
    wtab,
    pull,
    in_sem,
    out_sem,
    edge_sem,
    land_sem,
    send_sem,
):
    c = lax.axis_index("circ")
    s = lax.axis_index("span")
    blocks = 2 * ring

    def circ(shift):
        return {"circ": lax.rem(c + (shift + ring), ring)}

    def span(shift):
        return {"span": lax.rem(s + (shift + band), band)}

    def remote(source, target, sent, landed, where):
        return pltpu.make_async_remote_copy(
            src_ref=source,
            dst_ref=target,
            send_sem=sent,
            recv_sem=landed,
            device_id=where,
            device_id_type=pl.DeviceIdType.MESH,
        )

    loads = [
        (adj_s, adj.at[1]),
        (adj_r, adj.at[0]),
        (margin, lists),
        (count, live),
        (off_s, off.at[1]),
        (diag_s, diag.at[1]),
        (src_s, src.at[1]),
        (off_r, off.at[0]),
        (diag_r, diag.at[0]),
        (src_r, src.at[0]),
        (rstate, pick),
        (weight, wts),
    ]
    copies = [pltpu.make_async_copy(a, b, in_sem.at[i]) for i, (a, b) in enumerate(loads)]
    for one in copies:
        one.start()

    barrier = pltpu.get_barrier_semaphore()

    def greet(where):
        pl.semaphore_signal(
            barrier, inc=1, device_id=where, device_id_type=pl.DeviceIdType.MESH
        )

    far = [x for x in range(OFFSET, ring, STRIDE) if REACH < x < ring - REACH]
    for shift in far + list(range(1, REACH + 1)) + list(range(-REACH, 0)):
        greet(circ(shift))
    greet(span(1))
    greet(span(-1))

    def coarse(piece, landing, sign, n):
        @pl.loop(0, COARSE)
        def _(a):
            away = sign * (STRIDE * a + OFFSET)
            remote(piece, landing.at[a], send_sem.at[n], land_sem.at[n], circ(away)).start()

    def fine(piece, landing, sign, n):
        @pl.loop(1, REACH + 1)
        def _(t):
            remote(piece, landing.at[t], send_sem.at[n], land_sem.at[n], circ(sign * t)).start()
            low = landing.at[SLOTS - t]
            remote(piece, low, send_sem.at[n], land_sem.at[n], circ(-sign * t)).start()

    def drain(view, sem):
        pltpu.make_async_copy(view, view, sem).wait()

    def edges(source, step, field):
        lower = source.at[field, :, :, :, pl.ds(0, 128)]
        upper = source.at[field, :, :, :, pl.ds(128, 128)]
        sems = edge_sem.at[step, field]
        return [
            remote(upper, edge.at[step, 0, field], sems.at[4], sems.at[0], circ(1)),
            remote(lower, edge.at[step, 1, field], sems.at[5], sems.at[1], circ(-1)),
            remote(
                source.at[field, :, 1], rows.at[step, 0, field], sems.at[6], sems.at[2], span(1)
            ),
            remote(
                source.at[field, :, 0], rows.at[step, 1, field], sems.at[7], sems.at[3], span(-1)
            ),
        ]

    def begin(copies):
        for one in copies:
            one.start()
        return copies

    def finish(copies):
        for one in copies:
            one.wait()

    def front(target, source, row, half):
        target[half, :, row : row + 1, :] = source[1, :, row, 0:1, pl.ds(half * 128, 128)]

    pieces = [(row, half) for row in range(2) for half in range(2)]
    pad[...] = jnp.zeros_like(pad)
    qtab[...] = jnp.zeros_like(qtab)
    ptab[...] = jnp.zeros_like(ptab)
    wtab[...] = jnp.zeros_like(wtab)
    copies[0].wait()
    for row, half in pieces:
        front(sent_f.at[0], adj, row, half)
    copies[1].wait()
    pl.semaphore_wait(barrier, len(far) + 2 * REACH + 2)

    coarse(rstate, near_a, -1, 0)
    coarse(sent_f.at[0], far_a0, 1, 1)
    edges0_s = begin(edges(adj, 0, 1))

    @pl.loop(1, BESIDE + 1)
    def _(u):
        remote(rstate, home.at[u], send_sem.at[6], land_sem.at[6], circ(-u)).start()
        remote(rstate, home.at[HOMES - u], send_sem.at[6], land_sem.at[6], circ(u)).start()

    edges0_r = begin(edges(adj, 0, 0))

    def local_part(x, field):
        pad[field, :, :, 1:5, :] = x[...]
        value = diag[field] * x[...] - src[field]
        value = value - COUPLING * (pad[field, :, :, 0:4, :] + pad[field, :, :, 2:6, :])

        def add(w, total):
            return total + off[field, w].astype(jnp.float32) * x[w][None]

        part[field] = lax.fori_loop(0, off.shape[1], add, value)

    lane = lax.broadcasted_iota(jnp.int32, (1, 1, 1, 128), 3)
    below = jnp.where(s == 0, 0.0, 1.0).astype(jnp.float32)
    above = jnp.where(s == band - 1, 0.0, 1.0).astype(jnp.float32)

    def advance(x, result, field, step):
        for half in range(2):
            here = pl.ds(half * 128, 128)
            other = pl.ds(128 - half * 128, 128)
            mine = x[:, :, :, here]
            before = edge[step, 0, field] if half == 0 else x[:, :, :, other]
            after = x[:, :, :, other] if half == 0 else edge[step, 1, field]
            left = pltpu.roll(jnp.where(lane == 127, before, mine), 1, axis=3)
            right = pltpu.roll(jnp.where(lane == 0, after, mine), 127, axis=3)
            beside = left + right
            spanwise0 = rows[step, 0, field, :, :, here] * below + x[:, 1, :, here]
            spanwise1 = rows[step, 1, field, :, :, here] * above + x[:, 0, :, here]
            whole = part[field, :, :, :, here] - COUPLING * beside
            result[:, 0, :, here] = mine[:, 0] - STEP_SIZE * (whole[:, 0] - COUPLING * spanwise0)
            result[:, 1, :, here] = mine[:, 1] - STEP_SIZE * (whole[:, 1] - COUPLING * spanwise1)

    for one in copies[4:7]:
        one.wait()
    local_part(adj.at[1], 1)
    finish(edges0_s)
    advance(adj.at[1], adj1.at[1], 1, 0)
    for row, half in pieces:
        front(sent_f.at[1], adj1, row, half)
    coarse(sent_f.at[1], far_a1, 1, 2)

    copies[2].wait()
    copies[3].wait()
    start = lists[0, 0, 0]

    def lowest(b, least):
        for row in range(2):
            e = ((lists[row, 0, b] - b - 4 * row - start + 2 + blocks) & (blocks - 1)) - 2
            least = jnp.minimum(least, e)
        return least

    base = (start + lax.fori_loop(0, blocks, lowest, jnp.int32(0)) + blocks) & (blocks - 1)
    shift = lax.shift_right_logical(base, 1) + 3
    fine_at = ((shift - 1) & 7) - 3
    coarse_at = lax.shift_right_logical(shift - fine_at - OFFSET, 3) & 7

    drain(near_a, land_sem.at[0])
    chosen = near_a[coarse_at]
    sent_n[...] = chosen
    near_b[0] = chosen
    fine(sent_n, near_b, -1, 3)
    drain(far_a0, land_sem.at[1])
    chosen = far_a0[coarse_at]
    sent_f[2] = chosen
    far_b0[0] = chosen
    fine(sent_f.at[2], far_b0, 1, 4)

    for one in copies[7:]:
        one.wait()
    local_part(adj.at[0], 0)
    finish(edges0_r)
    advance(adj.at[0], adj1.at[0], 0, 0)

    def wrap(t, size):
        t = t + (size & lax.shift_right_arithmetic(t, 31))
        return jnp.minimum(t, size - 1)

    def masked(factor, k, alive):
        shape = factor.shape
        return jnp.where(jnp.full(shape, k) < jnp.full(shape, alive), factor, 0.0)

    home[0] = pick[...]
    drain(home.at[pl.ds(1, HOMES - 1)], land_sem.at[6])
    for half in range(2):
        home_f[:, half] = home[:, :, :, pl.ds(half * 128, 128)].astype(jnp.float32)

    places = [(row, i) for row in range(2) for i in range(SEEN)]
    owners = []
    for row, i in places:
        b = (2 * c + 1 - base - 4 * row - i + 2 * blocks) & (blocks - 1)
        owners.append(b)
        first = lists[row, 0, b]
        alive = live[row, b]
        total = jnp.zeros((6, 1, 128), jnp.float32)
        for k in range(4):
            near = (first + k - 2 * c + 2 * BESIDE + blocks) & (blocks - 1)
            u = wrap(lax.shift_right_logical(near, 1) - BESIDE, HOMES)
            got = home_f[u, near & 1, :, row : row + 1, :]
            total = total + masked(wts[row, b, k : k + 1, :], k, alive)[None] * got
        qtab[row, :, i : i + 1, :] = total
        for block in range(2):
            if not 0 <= i - 1 + block < SEEN - 1:
                continue
            k = (2 * c + block - first + blocks) & (blocks - 1)
            factor = wts[row, b, pl.ds(jnp.minimum(k, 3), 1), :]
            wtab[row, block, i : i + 1, :] = masked(factor, k, alive)

    drain(far_a1, land_sem.at[2])
    chosen = far_a1[coarse_at]
    sent_f[3] = chosen
    far_b1[0] = chosen
    fine(sent_f.at[3], far_b1, 1, 5)

    def gather(landing):
        for (row, i), b in zip(places, owners):
            delta = (b - 2 * c + 2 * shift + 4 + blocks) & (blocks - 1)
            slot = wrap(fine_at - lax.shift_right_logical(delta, 1) + 2, SLOTS)
            ptab[row, :, i : i + 1, :] = landing[slot, delta & 1, :, row : row + 1, :]

    def speeds_of(q):
        return jnp.sqrt(1.0 + q * q)

    def interface_flux(q, p, axis):
        projection = jnp.sum(q * p, axis=axis, keepdims=True)
        projection = projection / (6.0 + jnp.sum(q * q, axis=axis, keepdims=True))
        return speeds_of(q) * p + 0.5 * q * projection

    def pulled(value):
        wire = value.astype(jnp.bfloat16).astype(jnp.float32)
        for row in range(2):
            for block in range(2):
                total = jnp.sum(wtab[row, block][None] * wire[row], axis=1, keepdims=True)
                pull[:, row : row + 1, pl.ds(block * 128, 128)] = total

    drain(far_b0.at[pl.ds(1, SLOTS - 1)], land_sem.at[4])
    gather(far_b0)
    first_flux = interface_flux(qtab[...], ptab[...], 1)
    pulled(first_flux)
    for row in range(2):
        adj1[0, :, row, 3:4, :] = adj1[0, :, row, 3:4, :] + STEP_SIZE * pull[:, row : row + 1, :]
    edges1_r = begin(edges(adj1, 1, 0))
    ptab[...] = STEP_SIZE * first_flux
    qtab1 = qtab

    drain(near_b.at[pl.ds(1, SLOTS - 1)], land_sem.at[3])
    for half in range(2):
        near_f[:, half] = near_b[:, :, :, pl.ds(half * 128, 128)].astype(jnp.float32)
    for row in range(2):
        for block in range(2):
            b = 2 * c + block
            first = lists[row, 0, b]
            alive = live[row, b]
            total = jnp.zeros((6, 1, 128), jnp.float32)
            for k in range(4):
                delta = (first + k - 2 * c - 2 * shift + 6 + 2 * blocks) & (blocks - 1)
                slot = wrap(fine_at + lax.shift_right_logical(delta, 1) - 3, SLOTS)
                got = near_f[slot, delta & 1, :, row : row + 1, :]
                total = total + masked(wts[row, b, k : k + 1, :], k, alive)[None] * got
            prim[:, row : row + 1, pl.ds(block * 128, 128)] = total
    for row in range(2):
        face[:, row : row + 1, :] = adj[1, :, row, 0:1, :]
    value = STEP_SIZE * interface_flux(prim[...], face[...], 0)
    flux[...] = value
    for row in range(2):
        moved = adj1[1, :, row, 0:1, :] - flux[:, row : row + 1, :]
        adj1[1, :, row, 0:1, :] = moved
        face[:, row : row + 1, :] = moved
    edges1_s = begin(edges(adj1, 1, 1))
    flux[...] = STEP_SIZE * interface_flux(prim[...], face[...], 0)

    local_part(adj1.at[0], 0)
    local_part(adj1.at[1], 1)

    finish(edges1_s)
    advance(adj1.at[1], adj.at[1], 1, 1)
    for row in range(2):
        adj[1, :, row, 0:1, :] = adj[1, :, row, 0:1, :] - flux[:, row : row + 1, :]
    store_s = pltpu.make_async_copy(adj.at[1], out_s, out_sem.at[0])
    store_s.start()

    finish(edges1_r)
    advance(adj1.at[0], adj.at[0], 0, 1)
    scaled = ptab[...]
    drain(far_b1.at[pl.ds(1, SLOTS - 1)], land_sem.at[5])
    gather(far_b1)
    pulled(interface_flux(qtab1[...], ptab[...] - scaled, 1))
    for row in range(2):
        adj[0, :, row, 3:4, :] = adj[0, :, row, 3:4, :] + STEP_SIZE * pull[:, row : row + 1, :]
    store_r = pltpu.make_async_copy(adj.at[0], out_r, out_sem.at[1])
    store_r.start()

    drain(near_a, send_sem.at[0])
    drain(far_a0, send_sem.at[1])
    drain(far_a1, send_sem.at[2])
    drain(near_b.at[pl.ds(1, SLOTS - 1)], send_sem.at[3])
    drain(far_b0.at[pl.ds(1, SLOTS - 1)], send_sem.at[4])
    drain(far_b1.at[pl.ds(1, SLOTS - 1)], send_sem.at[5])
    drain(home.at[pl.ds(1, HOMES - 1)], send_sem.at[6])
    store_s.wait()
    store_r.wait()


def solution(mesh):
    ring, band = mesh.shape["circ"], mesh.shape["span"]

    def per_device(
        adjoint_rotor,
        adjoint_stator,
        jac_diag_rotor,
        jac_diag_stator,
        jac_off_rotor,
        jac_off_stator,
        source_rotor,
        source_stator,
        rotor_state,
        margin_block,
        face_count,
        margin_weight,
    ):
        f32, bf16 = jnp.float32, jnp.bfloat16
        shape = adjoint_rotor.shape
        piece = rotor_state.shape
        split = (2, 6, 2, 128)
        lists = jnp.transpose(margin_block, (0, 2, 1))
        out = jax.ShapeDtypeStruct(shape, f32)
        hbm = pl.BlockSpec(memory_space=pltpu.HBM)
        return pl.pallas_call(
            functools.partial(kernel, ring, band),
            out_shape=(out, out),
            in_specs=[hbm] * 12,
            out_specs=(hbm, hbm),
            scratch_shapes=[
                pltpu.VMEM((2,) + shape, f32),
                pltpu.VMEM((2,) + shape, f32),
                pltpu.VMEM((2,) + jac_off_rotor.shape, bf16),
                pltpu.VMEM((2,) + shape, f32),
                pltpu.VMEM(margin_weight.shape, f32),
                pltpu.SMEM(lists.shape, jnp.int32),
                pltpu.SMEM(face_count.shape, jnp.int32),
                pltpu.VMEM(piece, bf16),
                pltpu.VMEM((2, 6, 2, 8, 256), f32),
                pltpu.VMEM((2,) + shape, f32),
                pltpu.VMEM((2,) + shape, f32),
                pltpu.VMEM((STEPS, 2, 2, 6, 2, 4, 128), f32),
                pltpu.VMEM((STEPS, 2, 2, 6, 4, 256), f32),
                pltpu.VMEM((HOMES,) + piece, bf16),
                pltpu.VMEM((HOMES,) + split, f32),
                pltpu.VMEM((COARSE,) + piece, bf16),
                pltpu.VMEM((SLOTS,) + piece, bf16),
                pltpu.VMEM((SLOTS,) + split, f32),
                pltpu.VMEM(piece, bf16),
                pltpu.VMEM(piece, f32),
                pltpu.VMEM(piece, f32),
                pltpu.VMEM(piece, f32),
                pltpu.VMEM((COARSE,) + split, f32),
                pltpu.VMEM((COARSE,) + split, f32),
                pltpu.VMEM((SLOTS,) + split, f32),
                pltpu.VMEM((SLOTS,) + split, f32),
                pltpu.VMEM((4,) + split, f32),
                pltpu.VMEM((2, 6, 8, 128), f32),
                pltpu.VMEM((2, 6, 8, 128), f32),
                pltpu.VMEM((2, 2, 8, 128), f32),
                pltpu.VMEM(piece, f32),
                pltpu.SemaphoreType.DMA((12,)),
                pltpu.SemaphoreType.DMA((2,)),
                pltpu.SemaphoreType.DMA((STEPS, 2, 8)),
                pltpu.SemaphoreType.DMA((7,)),
                pltpu.SemaphoreType.DMA((7,)),
            ],
            compiler_params=pltpu.CompilerParams(
                collective_id=0, has_side_effects=True, vmem_limit_bytes=60 * 1024 * 1024
            ),
            name="sweep",
        )(
            adjoint_rotor,
            adjoint_stator,
            jac_diag_rotor,
            jac_diag_stator,
            jac_off_rotor,
            jac_off_stator,
            source_rotor,
            source_stator,
            rotor_state,
            lists,
            face_count,
            margin_weight,
        )

    field = P(None, "span", None, "circ")
    matrix = P(None, None, "span", None, "circ")
    placed = (field,) * 4 + (matrix,) * 2 + (field,) * 2
    placed = placed + (
        P(None, "span", "circ"),
        P("span", None, None),
        P("span", None),
        P("span", None, None, None),
    )
    return jax.shard_map(
        per_device, mesh=mesh, in_specs=placed, out_specs=(field, field), check_vma=False
    )
```

time: 59.1 us -> 51.3 us (0.87)
  Pallas kernels: 56.1 us -> 48.4 us
    pallas_call x1, Pallas kernels: 56.1 us -> 48.4 us  [per_device(): pl.pallas_call(functools.partial(kernel, ring, band), out_shape=(out, out...]
where the time goes in v2:
time: 51.3 us; the launch traced here: 51.1 us
  Pallas kernels  48.4 us (94%)
  local copies, waits for them, and re-layouts  2.06 us (4%)
  between operations  0.65 us (1%)
    pallas_call x1, Pallas kernels, per_device(): pl.pallas_call(functools.partial(kernel, ring, band), out_shape=(out, out...  48.4 us
    unnamed x4, local copies, waits for them, and re-layouts  2.06 us

profile of v2, /device:TPU:1, one launch (start us, length us, event | category | flops | bytes accessed | tf_op | source)
XLA Modules:
  0.0 51.1 jit_solution(2134059673476923680)
XLA Ops:
  0.6 48.4 %sweep.1 = (f32[6,2,4,256]{3,2,1,0:T(4,128)}, f32[6,2,4,256]{3,2,1,0:T(4,128)}) custom-call(f32[6,2,4,256]{3,2,1,0:T(4,128)} %adj_r.1, f32[6,2,4,256]{3,2,1,0:T(4,128)} %adj_s.1, f32[6,2,4,256]{3,2,1,0:T(4,128)} %diag_r.1, f32[6,2,4,256]{3,2,1,0:T(4,128)} %diag_s.1, bf16[6,6,2,4,256]{4,3,2,1,0:T(4,128)(2,1)} %off_r.1, bf16[6,6,2,4,256]{4,3,2,1,0:T(4,128)(2,1)} %off_s.1, ...), custom_call_target="tpu_custom_call" | custom-call | tf_op jit(solution)/shard_map/sweep/pallas_call | solution.py:417
  49.0 0.0 copy-start
  49.0 1.4 %copy.16 = f32[6,2,4,256]{3,2,1,0:T(4,128)} copy(f32[6,2,4,256]{3,2,1,0:T(4,128)} %get-tuple-element.4) | data formatting | bytes 98304
  50.5 0.0 copy-done
  50.5 0.6 %copy.17 = f32[6,2,4,256]{3,2,1,0:T(4,128)} copy(f32[6,2,4,256]{3,2,1,0:T(4,128)S(1)} %copy-done) | data formatting | bytes 98304
Async XLA Ops:
  49.0 1.4 %copy-start = (f32[6,2,4,256]{3,2,1,0:T(4,128)S(1)}, f32[6,2,4,256]{3,2,1,0:T(4,128)}, u32[]{:S(2)}) copy-start(f32[6,2,4,256]{3,2,1,0:T(4,128)} %get-tuple-element.5) | copy-start | bytes 147460

commit v3 on v2

--- a/solution.py
+++ b/solution.py
@@ -15,6 +15,8 @@
 OFFSET = 4
 REACH = 6
 SLOTS = 2 * REACH + 1
+COMMON = 4
+FILLED = REACH + COMMON
 BESIDE = 3
 HOMES = 2 * BESIDE + 1
 SEEN = 7
@@ -64,8 +66,14 @@
     far_b0,
     far_b1,
     sent_f,
+    sent_d,
+    delta,
+    far_f,
+    side,
+    brow,
     qtab,
     ptab,
+    dtab,
     wtab,
     pull,
     in_sem,
@@ -73,6 +81,7 @@
     edge_sem,
     land_sem,
     send_sem,
+    tip_sem,
 ):
     c = lax.axis_index("circ")
     s = lax.axis_index("span")
@@ -93,6 +102,19 @@
             device_id=where,
             device_id_type=pl.DeviceIdType.MESH,
         )
+
+    barrier = pltpu.get_barrier_semaphore()
+
+    def greet(where):
+        pl.semaphore_signal(
+            barrier, inc=1, device_id=where, device_id_type=pl.DeviceIdType.MESH
+        )
+
+    far = [x for x in range(OFFSET, ring, STRIDE) if REACH < x < ring - REACH]
+    for shift in far + list(range(1, REACH + 1)) + list(range(-REACH, 0)):
+        greet(circ(shift))
+    greet(span(1))
+    greet(span(-1))
 
     loads = [
         (adj_s, adj.at[1]),
@@ -112,19 +134,6 @@
     for one in copies:
         one.start()
 
-    barrier = pltpu.get_barrier_semaphore()
-
-    def greet(where):
-        pl.semaphore_signal(
-            barrier, inc=1, device_id=where, device_id_type=pl.DeviceIdType.MESH
-        )
-
-    far = [x for x in range(OFFSET, ring, STRIDE) if REACH < x < ring - REACH]
-    for shift in far + list(range(1, REACH + 1)) + list(range(-REACH, 0)):
-        greet(circ(shift))
-    greet(span(1))
-    greet(span(-1))
-
     def coarse(piece, landing, sign, n):
         @pl.loop(0, COARSE)
         def _(a):
@@ -137,6 +146,22 @@
             remote(piece, landing.at[t], send_sem.at[n], land_sem.at[n], circ(sign * t)).start()
             low = landing.at[SLOTS - t]
             remote(piece, low, send_sem.at[n], land_sem.at[n], circ(-sign * t)).start()
+
+    def fine_rows(piece, landing, n):
+        def go(row, slot, away):
+            source = piece if row is None else piece.at[row]
+            target = landing.at[slot] if row is None else landing.at[slot, row]
+            remote(source, target, send_sem.at[n], land_sem.at[n], circ(away)).start()
+
+        @pl.loop(1, COMMON + 1)
+        def _(t):
+            go(None, t, t)
+            go(None, SLOTS - t, -t)
+
+        @pl.loop(COMMON + 1, REACH + 1)
+        def _(t):
+            go(1, t, t)
+            go(0, SLOTS - t, -t)
 
     def drain(view, sem):
         pltpu.make_async_copy(view, view, sem).wait()
@@ -166,12 +191,17 @@
             one.wait()
 
     def front(target, source, row, half):
-        target[half, :, row : row + 1, :] = source[1, :, row, 0:1, pl.ds(half * 128, 128)]
+        target[row, :, half : half + 1, :] = source[1, :, row, 0:1, pl.ds(half * 128, 128)]
 
     pieces = [(row, half) for row in range(2) for half in range(2)]
     pad[...] = jnp.zeros_like(pad)
     qtab[...] = jnp.zeros_like(qtab)
     ptab[...] = jnp.zeros_like(ptab)
+    dtab[...] = jnp.zeros_like(dtab)
+    for landing in (far_b0, far_b1):
+        for t in range(COMMON + 1, REACH + 1):
+            landing[t, 0] = jnp.zeros_like(landing[t, 0])
+            landing[SLOTS - t, 1] = jnp.zeros_like(landing[t, 0])
     wtab[...] = jnp.zeros_like(wtab)
     copies[0].wait()
     for row, half in pieces:
@@ -179,15 +209,24 @@
     copies[1].wait()
     pl.semaphore_wait(barrier, len(far) + 2 * REACH + 2)
 
+    first = sent_f.at[0]
+    tips = begin(
+        [
+            remote(first, side.at[0], tip_sem.at[4], tip_sem.at[0], circ(1)),
+            remote(first, side.at[1], tip_sem.at[5], tip_sem.at[1], circ(-1)),
+            remote(first.at[1], brow.at[0], tip_sem.at[6], tip_sem.at[2], span(1)),
+            remote(first.at[0], brow.at[1], tip_sem.at[7], tip_sem.at[3], span(-1)),
+        ]
+    )
+    coarse(first, far_a0, 1, 1)
     coarse(rstate, near_a, -1, 0)
-    coarse(sent_f.at[0], far_a0, 1, 1)
-    edges0_s = begin(edges(adj, 0, 1))
 
     @pl.loop(1, BESIDE + 1)
     def _(u):
         remote(rstate, home.at[u], send_sem.at[6], land_sem.at[6], circ(-u)).start()
         remote(rstate, home.at[HOMES - u], send_sem.at[6], land_sem.at[6], circ(u)).start()
 
+    edges0_s = begin(edges(adj, 0, 1))
     edges0_r = begin(edges(adj, 0, 0))
 
     def local_part(x, field):
@@ -223,11 +262,24 @@
     for one in copies[4:7]:
         one.wait()
     local_part(adj.at[1], 1)
-    finish(edges0_s)
-    advance(adj.at[1], adj1.at[1], 1, 0)
+    finish(tips)
+    line = lax.broadcasted_iota(jnp.int32, (1, 1, 128), 2)
     for row, half in pieces:
-        front(sent_f.at[1], adj1, row, half)
-    coarse(sent_f.at[1], far_a1, 1, 2)
+
+        def mine(row, half):
+            return sent_f[0, row, :, half : half + 1, :]
+
+        x = mine(row, half)
+        before = side[0, row, :, 1:2, :] if half == 0 else mine(row, 0)
+        after = mine(row, 1) if half == 0 else side[1, row, :, 0:1, :]
+        around = pltpu.roll(jnp.where(line == 127, before, x), 1, axis=2)
+        around = around + pltpu.roll(jnp.where(line == 0, after, x), 127, axis=2)
+        outer = brow[row, :, half : half + 1, :] * (below if row == 0 else above)
+        around = around + outer + mine(1 - row, half)
+        value = part[1, :, row, 0:1, pl.ds(half * 128, 128)] - COUPLING * around
+        delta[row, :, half : half + 1, :] = -STEP_SIZE * value
+    sent_d[0] = delta[...].astype(jnp.bfloat16)
+    coarse(sent_d.at[0], far_a1, 1, 2)
 
     copies[2].wait()
     copies[3].wait()
@@ -239,21 +291,24 @@
             least = jnp.minimum(least, e)
         return least
 
-    base = (start + lax.fori_loop(0, blocks, lowest, jnp.int32(0)) + blocks) & (blocks - 1)
+    base = (start + lax.fori_loop(0, blocks, lowest, jnp.int32(0), unroll=8) + blocks) & (blocks - 1)
     shift = lax.shift_right_logical(base, 1) + 3
     fine_at = ((shift - 1) & 7) - 3
     coarse_at = lax.shift_right_logical(shift - fine_at - OFFSET, 3) & 7
 
+    drain(far_a0, land_sem.at[1])
+    chosen = far_a0[coarse_at]
+    sent_f[1] = chosen
+    far_b0[0] = chosen
+    fine_rows(sent_f.at[1], far_b0, 4)
     drain(near_a, land_sem.at[0])
     chosen = near_a[coarse_at]
     sent_n[...] = chosen
     near_b[0] = chosen
     fine(sent_n, near_b, -1, 3)
-    drain(far_a0, land_sem.at[1])
-    chosen = far_a0[coarse_at]
-    sent_f[2] = chosen
-    far_b0[0] = chosen
-    fine(sent_f.at[2], far_b0, 1, 4)
+
+    finish(edges0_s)
+    advance(adj.at[1], adj1.at[1], 1, 0)
 
     for one in copies[7:]:
         one.wait()
@@ -297,15 +352,15 @@
 
     drain(far_a1, land_sem.at[2])
     chosen = far_a1[coarse_at]
-    sent_f[3] = chosen
+    sent_d[1] = chosen
     far_b1[0] = chosen
-    fine(sent_f.at[3], far_b1, 1, 5)
-
-    def gather(landing):
+    fine_rows(sent_d.at[1], far_b1, 5)
+
+    def gather(landing, table):
         for (row, i), b in zip(places, owners):
             delta = (b - 2 * c + 2 * shift + 4 + blocks) & (blocks - 1)
             slot = wrap(fine_at - lax.shift_right_logical(delta, 1) + 2, SLOTS)
-            ptab[row, :, i : i + 1, :] = landing[slot, delta & 1, :, row : row + 1, :]
+            table[row, :, i : i + 1, :] = landing[slot, row, :, pl.ds(delta & 1, 1), :]
 
     def speeds_of(q):
         return jnp.sqrt(1.0 + q * q)
@@ -322,15 +377,14 @@
                 total = jnp.sum(wtab[row, block][None] * wire[row], axis=1, keepdims=True)
                 pull[:, row : row + 1, pl.ds(block * 128, 128)] = total
 
-    drain(far_b0.at[pl.ds(1, SLOTS - 1)], land_sem.at[4])
-    gather(far_b0)
+    drain(far_b0.at[pl.ds(1, FILLED)], land_sem.at[4])
+    gather(far_b0, ptab)
     first_flux = interface_flux(qtab[...], ptab[...], 1)
     pulled(first_flux)
     for row in range(2):
         adj1[0, :, row, 3:4, :] = adj1[0, :, row, 3:4, :] + STEP_SIZE * pull[:, row : row + 1, :]
     edges1_r = begin(edges(adj1, 1, 0))
-    ptab[...] = STEP_SIZE * first_flux
-    qtab1 = qtab
+    ptab[...] = ptab[...] - STEP_SIZE * first_flux
 
     drain(near_b.at[pl.ds(1, SLOTS - 1)], land_sem.at[3])
     for half in range(2):
@@ -370,10 +424,10 @@
 
     finish(edges1_r)
     advance(adj1.at[0], adj.at[0], 0, 1)
-    scaled = ptab[...]
-    drain(far_b1.at[pl.ds(1, SLOTS - 1)], land_sem.at[5])
-    gather(far_b1)
-    pulled(interface_flux(qtab1[...], ptab[...] - scaled, 1))
+    drain(far_b1.at[pl.ds(1, FILLED)], land_sem.at[5])
+    far_f[...] = far_b1[...].astype(jnp.float32)
+    gather(far_f, dtab)
+    pulled(interface_flux(qtab[...], ptab[...] + dtab[...], 1))
     for row in range(2):
         adj[0, :, row, 3:4, :] = adj[0, :, row, 3:4, :] + STEP_SIZE * pull[:, row : row + 1, :]
     store_r = pltpu.make_async_copy(adj.at[0], out_r, out_sem.at[1])
@@ -383,8 +437,8 @@
     drain(far_a0, send_sem.at[1])
     drain(far_a1, send_sem.at[2])
     drain(near_b.at[pl.ds(1, SLOTS - 1)], send_sem.at[3])
-    drain(far_b0.at[pl.ds(1, SLOTS - 1)], send_sem.at[4])
-    drain(far_b1.at[pl.ds(1, SLOTS - 1)], send_sem.at[5])
+    drain(far_b0.at[pl.ds(1, FILLED)], send_sem.at[4])
+    drain(far_b1.at[pl.ds(1, FILLED)], send_sem.at[5])
     drain(home.at[pl.ds(1, HOMES - 1)], send_sem.at[6])
     store_s.wait()
     store_r.wait()
@@ -443,10 +497,16 @@
                 pltpu.VMEM(piece, f32),
                 pltpu.VMEM(piece, f32),
                 pltpu.VMEM((COARSE,) + split, f32),
-                pltpu.VMEM((COARSE,) + split, f32),
+                pltpu.VMEM((COARSE,) + split, bf16),
                 pltpu.VMEM((SLOTS,) + split, f32),
+                pltpu.VMEM((SLOTS,) + split, bf16),
+                pltpu.VMEM((2,) + split, f32),
+                pltpu.VMEM((2,) + split, bf16),
+                pltpu.VMEM(split, f32),
                 pltpu.VMEM((SLOTS,) + split, f32),
-                pltpu.VMEM((4,) + split, f32),
+                pltpu.VMEM((2,) + split, f32),
+                pltpu.VMEM((2,) + split[1:], f32),
+                pltpu.VMEM((2, 6, 8, 128), f32),
                 pltpu.VMEM((2, 6, 8, 128), f32),
                 pltpu.VMEM((2, 6, 8, 128), f32),
                 pltpu.VMEM((2, 2, 8, 128), f32),
@@ -456,6 +516,7 @@
                 pltpu.SemaphoreType.DMA((STEPS, 2, 8)),
                 pltpu.SemaphoreType.DMA((7,)),
                 pltpu.SemaphoreType.DMA((7,)),
+                pltpu.SemaphoreType.DMA((8,)),
             ],
             compiler_params=pltpu.CompilerParams(
                 collective_id=0, has_side_effects=True, vmem_limit_bytes=60 * 1024 * 1024

time: 51.3 us -> 48.8 us (0.951)
  Pallas kernels: 48.4 us -> 45.8 us
    pallas_call x1, Pallas kernels: 48.4 us -> 45.8 us  [per_device(): pl.pallas_call(functools.partial(kernel, ring, band), out_shape=(out, out...]
where the time goes in v3:
time: 48.8 us; the launch traced here: 48.5 us
  Pallas kernels  45.8 us (94%)
  local copies, waits for them, and re-layouts  2.06 us (4%)
  between operations  0.65 us (1%)
    pallas_call x1, Pallas kernels, per_device(): pl.pallas_call(functools.partial(kernel, ring, band), out_shape=(out, out...  45.8 us
    unnamed x4, local copies, waits for them, and re-layouts  2.06 us

profile of v3, /device:TPU:1, one launch (start us, length us, event | category | flops | bytes accessed | tf_op | source)
XLA Modules:
  0.0 48.5 jit_solution(5936439538244345226)
XLA Ops:
  0.6 45.8 %sweep.1 = (f32[6,2,4,256]{3,2,1,0:T(4,128)}, f32[6,2,4,256]{3,2,1,0:T(4,128)}) custom-call(f32[6,2,4,256]{3,2,1,0:T(4,128)} %adj_r.1, f32[6,2,4,256]{3,2,1,0:T(4,128)} %adj_s.1, f32[6,2,4,256]{3,2,1,0:T(4,128)} %diag_r.1, f32[6,2,4,256]{3,2,1,0:T(4,128)} %diag_s.1, bf16[6,6,2,4,256]{4,3,2,1,0:T(4,128)(2,1)} %off_r.1, bf16[6,6,2,4,256]{4,3,2,1,0:T(4,128)(2,1)} %off_s.1, ...), custom_call_target="tpu_custom_call" | custom-call | tf_op jit(solution)/shard_map/sweep/pallas_call | solution.py:471
  46.5 0.0 copy-start
  46.5 1.4 %copy.16 = f32[6,2,4,256]{3,2,1,0:T(4,128)} copy(f32[6,2,4,256]{3,2,1,0:T(4,128)} %get-tuple-element.4) | data formatting | bytes 98304
  47.9 0.0 copy-done
  47.9 0.6 %copy.17 = f32[6,2,4,256]{3,2,1,0:T(4,128)} copy(f32[6,2,4,256]{3,2,1,0:T(4,128)S(1)} %copy-done) | data formatting | bytes 98304
Async XLA Ops:
  46.5 1.4 %copy-start = (f32[6,2,4,256]{3,2,1,0:T(4,128)S(1)}, f32[6,2,4,256]{3,2,1,0:T(4,128)}, u32[]{:S(2)}) copy-start(f32[6,2,4,256]{3,2,1,0:T(4,128)} %get-tuple-element.5) | copy-start | bytes 147460

commit v4 on v3

--- a/solution.py
+++ b/solution.py
@@ -67,8 +67,6 @@
     far_b1,
     sent_f,
     sent_d,
-    delta,
-    far_f,
     side,
     brow,
     qtab,
@@ -221,14 +219,6 @@
     coarse(first, far_a0, 1, 1)
     coarse(rstate, near_a, -1, 0)
 
-    @pl.loop(1, BESIDE + 1)
-    def _(u):
-        remote(rstate, home.at[u], send_sem.at[6], land_sem.at[6], circ(-u)).start()
-        remote(rstate, home.at[HOMES - u], send_sem.at[6], land_sem.at[6], circ(u)).start()
-
-    edges0_s = begin(edges(adj, 0, 1))
-    edges0_r = begin(edges(adj, 0, 0))
-
     def local_part(x, field):
         pad[field, :, :, 1:5, :] = x[...]
         value = diag[field] * x[...] - src[field]
@@ -277,9 +267,17 @@
         outer = brow[row, :, half : half + 1, :] * (below if row == 0 else above)
         around = around + outer + mine(1 - row, half)
         value = part[1, :, row, 0:1, pl.ds(half * 128, 128)] - COUPLING * around
-        delta[row, :, half : half + 1, :] = -STEP_SIZE * value
-    sent_d[0] = delta[...].astype(jnp.bfloat16)
+        sent_d[0, row, :, half : half + 1, :] = -STEP_SIZE * value
     coarse(sent_d.at[0], far_a1, 1, 2)
+
+    @pl.loop(1, BESIDE + 1)
+    def _(u):
+        remote(rstate, home.at[u], send_sem.at[6], land_sem.at[6], circ(-u)).start()
+        remote(rstate, home.at[HOMES - u], send_sem.at[6], land_sem.at[6], circ(u)).start()
+
+    edges0_s = begin(edges(adj, 0, 1))
+    edges0_r = begin(edges(adj, 0, 0))
+
 
     copies[2].wait()
     copies[3].wait()
@@ -295,6 +293,10 @@
     shift = lax.shift_right_logical(base, 1) + 3
     fine_at = ((shift - 1) & 7) - 3
     coarse_at = lax.shift_right_logical(shift - fine_at - OFFSET, 3) & 7
+
+    for one in copies[7:]:
+        one.wait()
+    local_part(adj.at[0], 0)
 
     drain(far_a0, land_sem.at[1])
     chosen = far_a0[coarse_at]
@@ -306,15 +308,6 @@
     sent_n[...] = chosen
     near_b[0] = chosen
     fine(sent_n, near_b, -1, 3)
-
-    finish(edges0_s)
-    advance(adj.at[1], adj1.at[1], 1, 0)
-
-    for one in copies[7:]:
-        one.wait()
-    local_part(adj.at[0], 0)
-    finish(edges0_r)
-    advance(adj.at[0], adj1.at[0], 0, 0)
 
     def wrap(t, size):
         t = t + (size & lax.shift_right_arithmetic(t, 31))
@@ -355,6 +348,11 @@
     sent_d[1] = chosen
     far_b1[0] = chosen
     fine_rows(sent_d.at[1], far_b1, 5)
+
+    finish(edges0_s)
+    advance(adj.at[1], adj1.at[1], 1, 0)
+    finish(edges0_r)
+    advance(adj.at[0], adj1.at[0], 0, 0)
 
     def gather(landing, table):
         for (row, i), b in zip(places, owners):
@@ -425,8 +423,7 @@
     finish(edges1_r)
     advance(adj1.at[0], adj.at[0], 0, 1)
     drain(far_b1.at[pl.ds(1, FILLED)], land_sem.at[5])
-    far_f[...] = far_b1[...].astype(jnp.float32)
-    gather(far_f, dtab)
+    gather(far_b1, dtab)
     pulled(interface_flux(qtab[...], ptab[...] + dtab[...], 1))
     for row in range(2):
         adj[0, :, row, 3:4, :] = adj[0, :, row, 3:4, :] + STEP_SIZE * pull[:, row : row + 1, :]
@@ -442,6 +439,17 @@
     drain(home.at[pl.ds(1, HOMES - 1)], send_sem.at[6])
     store_s.wait()
     store_r.wait()
+
+
+def deliver(from_r, from_s, out_r, out_s, sem):
+    moves = [
+        pltpu.make_async_copy(from_r, out_r, sem.at[0]),
+        pltpu.make_async_copy(from_s, out_s, sem.at[1]),
+    ]
+    for one in moves:
+        one.start()
+    for one in moves:
+        one.wait()
 
 
 def solution(mesh):
@@ -468,7 +476,7 @@
         lists = jnp.transpose(margin_block, (0, 2, 1))
         out = jax.ShapeDtypeStruct(shape, f32)
         hbm = pl.BlockSpec(memory_space=pltpu.HBM)
-        return pl.pallas_call(
+        swept = pl.pallas_call(
             functools.partial(kernel, ring, band),
             out_shape=(out, out),
             in_specs=[hbm] * 12,
@@ -497,13 +505,11 @@
                 pltpu.VMEM(piece, f32),
                 pltpu.VMEM(piece, f32),
                 pltpu.VMEM((COARSE,) + split, f32),
-                pltpu.VMEM((COARSE,) + split, bf16),
+                pltpu.VMEM((COARSE,) + split, f32),
                 pltpu.VMEM((SLOTS,) + split, f32),
-                pltpu.VMEM((SLOTS,) + split, bf16),
+                pltpu.VMEM((SLOTS,) + split, f32),
                 pltpu.VMEM((2,) + split, f32),
-                pltpu.VMEM((2,) + split, bf16),
-                pltpu.VMEM(split, f32),
-                pltpu.VMEM((SLOTS,) + split, f32),
+                pltpu.VMEM((2,) + split, f32),
                 pltpu.VMEM((2,) + split, f32),
                 pltpu.VMEM((2,) + split[1:], f32),
                 pltpu.VMEM((2, 6, 8, 128), f32),
@@ -536,6 +542,15 @@
             face_count,
             margin_weight,
         )
+        return pl.pallas_call(
+            deliver,
+            out_shape=(out, out),
+            in_specs=[hbm] * 2,
+            out_specs=(hbm, hbm),
+            scratch_shapes=[pltpu.SemaphoreType.DMA((2,))],
+            compiler_params=pltpu.CompilerParams(vmem_limit_bytes=60 * 1024 * 1024),
+            name="deliver",
+        )(*swept)
 
     field = P(None, "span", None, "circ")
     matrix = P(None, None, "span", None, "circ")

time: 48.8 us -> 51.9 us (1.064)
  Pallas kernels: 45.8 us -> 51.1 us
  local copies, waits for them, and re-layouts: 2.06 us -> 0 us
    pallas_call x0 -> x1, Pallas kernels: none -> 4.1 us  [per_device(): pl.pallas_call(deliver, out_shape=(out, out), in_specs=[hbm] * 2, out_spe...]
    unnamed x4 -> x0, local copies, waits for them, and re-layouts: 2.06 us -> none
    pallas_call x1, Pallas kernels: 45.8 us -> 47 us  [per_device(): pl.pallas_call(functools.partial(kernel, ring, band), out_shape=(out, out...]
where the time goes in v4:
time: 51.9 us; the launch traced here: 51.7 us
  Pallas kernels  51.1 us (98%)
  between operations  0.64 us (1%)
    pallas_call x1, Pallas kernels, per_device(): pl.pallas_call(functools.partial(kernel, ring, band), out_shape=(out, out...  47 us
    pallas_call x1, Pallas kernels, per_device(): pl.pallas_call(deliver, out_shape=(out, out), in_specs=[hbm] * 2, out_spe...  4.1 us

profile of v4, /device:TPU:1, one launch (start us, length us, event | category | flops | bytes accessed | tf_op | source)
XLA Modules:
  0.0 51.7 jit_solution(12700099539507554497)
XLA Ops:
  0.6 47.0 %sweep.1 = (f32[6,2,4,256]{3,2,1,0:T(4,128)}, f32[6,2,4,256]{3,2,1,0:T(4,128)}) custom-call(f32[6,2,4,256]{3,2,1,0:T(4,128)} %adj_r.1, f32[6,2,4,256]{3,2,1,0:T(4,128)} %adj_s.1, f32[6,2,4,256]{3,2,1,0:T(4,128)} %diag_r.1, f32[6,2,4,256]{3,2,1,0:T(4,128)} %diag_s.1, bf16[6,6,2,4,256]{4,3,2,1,0:T(4,128)(2,1)} %off_r.1, bf16[6,6,2,4,256]{4,3,2,1,0:T(4,128)(2,1)} %off_s.1, ...), custom_call_target="tpu_custom_call" | custom-call | tf_op jit(solution)/shard_map/sweep/pallas_call | solution.py:479
  47.6 4.1 %deliver.1 = (f32[6,2,4,256]{3,2,1,0:T(4,128)}, f32[6,2,4,256]{3,2,1,0:T(4,128)}) custom-call(f32[6,2,4,256]{3,2,1,0:T(4,128)} %get-tuple-element.4.from_r, f32[6,2,4,256]{3,2,1,0:T(4,128)} %get-tuple-element.5.from_s), custom_call_target="tpu_custom_call" | custom-call | tf_op jit(solution)/shard_map/deliver/pallas_call | solution.py:545

commit v5 on v4

--- a/solution.py
+++ b/solution.py
@@ -73,13 +73,16 @@
     ptab,
     dtab,
     wtab,
-    pull,
+    late,
+    late_side,
+    late_row,
     in_sem,
     out_sem,
     edge_sem,
     land_sem,
     send_sem,
     tip_sem,
+    late_sem,
 ):
     c = lax.axis_index("circ")
     s = lax.axis_index("span")
@@ -100,19 +103,6 @@
             device_id=where,
             device_id_type=pl.DeviceIdType.MESH,
         )
-
-    barrier = pltpu.get_barrier_semaphore()
-
-    def greet(where):
-        pl.semaphore_signal(
-            barrier, inc=1, device_id=where, device_id_type=pl.DeviceIdType.MESH
-        )
-
-    far = [x for x in range(OFFSET, ring, STRIDE) if REACH < x < ring - REACH]
-    for shift in far + list(range(1, REACH + 1)) + list(range(-REACH, 0)):
-        greet(circ(shift))
-    greet(span(1))
-    greet(span(-1))
 
     loads = [
         (adj_s, adj.at[1]),
@@ -129,18 +119,31 @@
         (weight, wts),
     ]
     copies = [pltpu.make_async_copy(a, b, in_sem.at[i]) for i, (a, b) in enumerate(loads)]
-    for one in copies:
+    copies[0].start()
+
+    barrier = pltpu.get_barrier_semaphore()
+
+    def greet(where):
+        pl.semaphore_signal(
+            barrier, inc=1, device_id=where, device_id_type=pl.DeviceIdType.MESH
+        )
+
+    far = [x for x in range(OFFSET, ring, STRIDE) if REACH < x < ring - REACH]
+    for shift in far + list(range(1, REACH + 1)) + list(range(-REACH, 0)):
+        greet(circ(shift))
+    greet(span(1))
+    greet(span(-1))
+
+    for one in copies[1:]:
         one.start()
 
     def coarse(piece, landing, sign, n):
-        @pl.loop(0, COARSE)
-        def _(a):
+        for a in range(COARSE):
             away = sign * (STRIDE * a + OFFSET)
             remote(piece, landing.at[a], send_sem.at[n], land_sem.at[n], circ(away)).start()
 
     def fine(piece, landing, sign, n):
-        @pl.loop(1, REACH + 1)
-        def _(t):
+        for t in range(1, REACH + 1):
             remote(piece, landing.at[t], send_sem.at[n], land_sem.at[n], circ(sign * t)).start()
             low = landing.at[SLOTS - t]
             remote(piece, low, send_sem.at[n], land_sem.at[n], circ(-sign * t)).start()
@@ -151,13 +154,11 @@
             target = landing.at[slot] if row is None else landing.at[slot, row]
             remote(source, target, send_sem.at[n], land_sem.at[n], circ(away)).start()
 
-        @pl.loop(1, COMMON + 1)
-        def _(t):
+        for t in range(1, COMMON + 1):
             go(None, t, t)
             go(None, SLOTS - t, -t)
 
-        @pl.loop(COMMON + 1, REACH + 1)
-        def _(t):
+        for t in range(COMMON + 1, REACH + 1):
             go(1, t, t)
             go(0, SLOTS - t, -t)
 
@@ -270,8 +271,7 @@
         sent_d[0, row, :, half : half + 1, :] = -STEP_SIZE * value
     coarse(sent_d.at[0], far_a1, 1, 2)
 
-    @pl.loop(1, BESIDE + 1)
-    def _(u):
+    for u in range(1, BESIDE + 1):
         remote(rstate, home.at[u], send_sem.at[6], land_sem.at[6], circ(-u)).start()
         remote(rstate, home.at[HOMES - u], send_sem.at[6], land_sem.at[6], circ(u)).start()
 
@@ -353,6 +353,8 @@
     advance(adj.at[1], adj1.at[1], 1, 0)
     finish(edges0_r)
     advance(adj.at[0], adj1.at[0], 0, 0)
+    edges1_s = begin(edges(adj1, 1, 1))
+    edges1_r = begin(edges(adj1, 1, 0))
 
     def gather(landing, table):
         for (row, i), b in zip(places, owners):
@@ -368,20 +370,51 @@
         projection = projection / (6.0 + jnp.sum(q * q, axis=axis, keepdims=True))
         return speeds_of(q) * p + 0.5 * q * projection
 
-    def pulled(value):
+    def pulled(value, which):
         wire = value.astype(jnp.bfloat16).astype(jnp.float32)
         for row in range(2):
             for block in range(2):
                 total = jnp.sum(wtab[row, block][None] * wire[row], axis=1, keepdims=True)
-                pull[:, row : row + 1, pl.ds(block * 128, 128)] = total
+                late[which, row, :, block : block + 1, :] = STEP_SIZE * total
+
+    def corrections(field):
+        piece, sems = late.at[field], late_sem.at[field]
+        return [
+            remote(piece, late_side.at[field, 0], sems.at[4], sems.at[0], circ(1)),
+            remote(piece, late_side.at[field, 1], sems.at[5], sems.at[1], circ(-1)),
+            remote(piece.at[1], late_row.at[field, 0], sems.at[6], sems.at[2], span(1)),
+            remote(piece.at[0], late_row.at[field, 1], sems.at[7], sems.at[3], span(-1)),
+        ]
+
+    def correct(target, field, layer, which):
+        for row, half in pieces:
+            lanes = pl.ds(half * 128, 128)
+            old = target[field, :, row, layer : layer + 1, lanes]
+            new = old + late[which, row, :, half : half + 1, :]
+            target[field, :, row, layer : layer + 1, lanes] = new
+
+    def settle(early, late_copies, field, layer):
+        for one in early:
+            one.wait_recv()
+        finish(late_copies)
+        for row, end in pieces:
+            old = edge[1, end, field, :, row, layer : layer + 1, :]
+            new = old + late_side[field, end, row, :, 1 - end : 2 - end, :]
+            edge[1, end, field, :, row, layer : layer + 1, :] = new
+        for end, half in pieces:
+            lanes = pl.ds(half * 128, 128)
+            old = rows[1, end, field, :, layer : layer + 1, lanes]
+            new = old + late_row[field, end, :, half : half + 1, :]
+            rows[1, end, field, :, layer : layer + 1, lanes] = new
 
     drain(far_b0.at[pl.ds(1, FILLED)], land_sem.at[4])
     gather(far_b0, ptab)
     first_flux = interface_flux(qtab[...], ptab[...], 1)
-    pulled(first_flux)
-    for row in range(2):
-        adj1[0, :, row, 3:4, :] = adj1[0, :, row, 3:4, :] + STEP_SIZE * pull[:, row : row + 1, :]
-    edges1_r = begin(edges(adj1, 1, 0))
+    pulled(first_flux, 0)
+    late_r = begin(corrections(0))
+    for one in edges1_r:
+        one.wait_send()
+    correct(adj1, 0, 3, 0)
     ptab[...] = ptab[...] - STEP_SIZE * first_flux
 
     drain(near_b.at[pl.ds(1, SLOTS - 1)], land_sem.at[3])
@@ -403,30 +436,33 @@
         face[:, row : row + 1, :] = adj[1, :, row, 0:1, :]
     value = STEP_SIZE * interface_flux(prim[...], face[...], 0)
     flux[...] = value
+    for row, half in pieces:
+        late[1, row, :, half : half + 1, :] = -flux[:, row : row + 1, pl.ds(half * 128, 128)]
+    late_s = begin(corrections(1))
+    for one in edges1_s:
+        one.wait_send()
     for row in range(2):
         moved = adj1[1, :, row, 0:1, :] - flux[:, row : row + 1, :]
         adj1[1, :, row, 0:1, :] = moved
         face[:, row : row + 1, :] = moved
-    edges1_s = begin(edges(adj1, 1, 1))
     flux[...] = STEP_SIZE * interface_flux(prim[...], face[...], 0)
 
     local_part(adj1.at[0], 0)
     local_part(adj1.at[1], 1)
 
-    finish(edges1_s)
+    settle(edges1_s, late_s, 1, 0)
     advance(adj1.at[1], adj.at[1], 1, 1)
     for row in range(2):
         adj[1, :, row, 0:1, :] = adj[1, :, row, 0:1, :] - flux[:, row : row + 1, :]
     store_s = pltpu.make_async_copy(adj.at[1], out_s, out_sem.at[0])
     store_s.start()
 
-    finish(edges1_r)
+    settle(edges1_r, late_r, 0, 3)
     advance(adj1.at[0], adj.at[0], 0, 1)
     drain(far_b1.at[pl.ds(1, FILLED)], land_sem.at[5])
     gather(far_b1, dtab)
-    pulled(interface_flux(qtab[...], ptab[...] + dtab[...], 1))
-    for row in range(2):
-        adj[0, :, row, 3:4, :] = adj[0, :, row, 3:4, :] + STEP_SIZE * pull[:, row : row + 1, :]
+    pulled(interface_flux(qtab[...], ptab[...] + dtab[...], 1), 2)
+    correct(adj, 0, 3, 2)
     store_r = pltpu.make_async_copy(adj.at[0], out_r, out_sem.at[1])
     store_r.start()
 
@@ -441,14 +477,21 @@
     store_r.wait()
 
 
-def deliver(from_r, from_s, out_r, out_s, sem):
-    moves = [
-        pltpu.make_async_copy(from_r, out_r, sem.at[0]),
-        pltpu.make_async_copy(from_s, out_s, sem.at[1]),
+def deliver(from_r, from_s, out_r, out_s, held, sem):
+    fetch = [
+        pltpu.make_async_copy(from_r, held.at[0], sem.at[0]),
+        pltpu.make_async_copy(from_s, held.at[1], sem.at[1]),
     ]
-    for one in moves:
+    store = [
+        pltpu.make_async_copy(held.at[0], out_r, sem.at[2]),
+        pltpu.make_async_copy(held.at[1], out_s, sem.at[3]),
+    ]
+    for one in fetch:
         one.start()
-    for one in moves:
+    for one, after in zip(fetch, store):
+        one.wait()
+        after.start()
+    for one in store:
         one.wait()
 
 
@@ -516,13 +559,16 @@
                 pltpu.VMEM((2, 6, 8, 128), f32),
                 pltpu.VMEM((2, 6, 8, 128), f32),
                 pltpu.VMEM((2, 2, 8, 128), f32),
-                pltpu.VMEM(piece, f32),
+                pltpu.VMEM((3,) + split, f32),
+                pltpu.VMEM((2, 2) + split, f32),
+                pltpu.VMEM((2, 2) + split[1:], f32),
                 pltpu.SemaphoreType.DMA((12,)),
                 pltpu.SemaphoreType.DMA((2,)),
                 pltpu.SemaphoreType.DMA((STEPS, 2, 8)),
                 pltpu.SemaphoreType.DMA((7,)),
                 pltpu.SemaphoreType.DMA((7,)),
                 pltpu.SemaphoreType.DMA((8,)),
+                pltpu.SemaphoreType.DMA((2, 8)),
             ],
             compiler_params=pltpu.CompilerParams(
                 collective_id=0, has_side_effects=True, vmem_limit_bytes=60 * 1024 * 1024
@@ -547,7 +593,7 @@
             out_shape=(out, out),
             in_specs=[hbm] * 2,
             out_specs=(hbm, hbm),
-            scratch_shapes=[pltpu.SemaphoreType.DMA((2,))],
+            scratch_shapes=[pltpu.VMEM((2,) + shape, f32), pltpu.SemaphoreType.DMA((4,))],
             compiler_params=pltpu.CompilerParams(vmem_limit_bytes=60 * 1024 * 1024),
             name="deliver",
         )(*swept)

time: 51.9 us -> 49.4 us (0.952)
  Pallas kernels: 51.1 us -> 48.5 us
    pallas_call x1, Pallas kernels: 4.1 us -> 1.48 us  [per_device(): pl.pallas_call(deliver, out_shape=(out, out), in_specs=[hbm] * 2, out_spe...]
where the time goes in v5:
time: 49.4 us; the launch traced here: 49.1 us
  Pallas kernels  48.5 us (98%)
  between operations  0.64 us (1%)
    pallas_call x1, Pallas kernels, per_device(): pl.pallas_call(functools.partial(kernel, ring, band), out_shape=(out, out...  47 us
    pallas_call x1, Pallas kernels, per_device(): pl.pallas_call(deliver, out_shape=(out, out), in_specs=[hbm] * 2, out_spe...  1.48 us

profile of v5, /device:TPU:1, one launch (start us, length us, event | category | flops | bytes accessed | tf_op | source)
XLA Modules:
  0.0 49.1 jit_solution(11792820620290370621)
XLA Ops:
  0.6 47.0 %sweep.1 = (f32[6,2,4,256]{3,2,1,0:T(4,128)}, f32[6,2,4,256]{3,2,1,0:T(4,128)}) custom-call(f32[6,2,4,256]{3,2,1,0:T(4,128)} %adj_r.1, f32[6,2,4,256]{3,2,1,0:T(4,128)} %adj_s.1, f32[6,2,4,256]{3,2,1,0:T(4,128)} %diag_r.1, f32[6,2,4,256]{3,2,1,0:T(4,128)} %diag_s.1, bf16[6,6,2,4,256]{4,3,2,1,0:T(4,128)(2,1)} %off_r.1, bf16[6,6,2,4,256]{4,3,2,1,0:T(4,128)(2,1)} %off_s.1, ...), custom_call_target="tpu_custom_call" | custom-call | tf_op jit(solution)/shard_map/sweep/pallas_call | solution.py:522
  47.7 1.5 %deliver.1 = (f32[6,2,4,256]{3,2,1,0:T(4,128)}, f32[6,2,4,256]{3,2,1,0:T(4,128)}) custom-call(f32[6,2,4,256]{3,2,1,0:T(4,128)} %get-tuple-element.4.from_r, f32[6,2,4,256]{3,2,1,0:T(4,128)} %get-tuple-element.5.from_s), custom_call_target="tpu_custom_call" | custom-call | tf_op jit(solution)/shard_map/deliver/pallas_call | solution.py:591

commit v6 on v5

--- a/solution.py
+++ b/solution.py
@@ -13,6 +13,7 @@
 COARSE = 8
 STRIDE = 8
 OFFSET = 4
+FAR_FIRST = (5, 6, 1, 2, 4, 7, 0, 3)
 REACH = 6
 SLOTS = 2 * REACH + 1
 COMMON = 4
@@ -128,7 +129,8 @@
             barrier, inc=1, device_id=where, device_id_type=pl.DeviceIdType.MESH
         )
 
-    far = [x for x in range(OFFSET, ring, STRIDE) if REACH < x < ring - REACH]
+    far = [STRIDE * a + OFFSET for a in FAR_FIRST]
+    far = [x for x in far if REACH < x < ring - REACH]
     for shift in far + list(range(1, REACH + 1)) + list(range(-REACH, 0)):
         greet(circ(shift))
     greet(span(1))
@@ -138,12 +140,12 @@
         one.start()
 
     def coarse(piece, landing, sign, n):
-        for a in range(COARSE):
+        for a in FAR_FIRST:
             away = sign * (STRIDE * a + OFFSET)
             remote(piece, landing.at[a], send_sem.at[n], land_sem.at[n], circ(away)).start()
 
     def fine(piece, landing, sign, n):
-        for t in range(1, REACH + 1):
+        for t in range(REACH, 0, -1):
             remote(piece, landing.at[t], send_sem.at[n], land_sem.at[n], circ(sign * t)).start()
             low = landing.at[SLOTS - t]
             remote(piece, low, send_sem.at[n], land_sem.at[n], circ(-sign * t)).start()
@@ -154,13 +156,13 @@
             target = landing.at[slot] if row is None else landing.at[slot, row]
             remote(source, target, send_sem.at[n], land_sem.at[n], circ(away)).start()
 
-        for t in range(1, COMMON + 1):
+        for t in range(REACH, COMMON, -1):
+            go(1, t, t)
+            go(0, SLOTS - t, -t)
+
+        for t in range(COMMON, 0, -1):
             go(None, t, t)
             go(None, SLOTS - t, -t)
-
-        for t in range(COMMON + 1, REACH + 1):
-            go(1, t, t)
-            go(0, SLOTS - t, -t)
 
     def drain(view, sem):
         pltpu.make_async_copy(view, view, sem).wait()

time: 49.4 us -> 48.9 us (0.990)
  Pallas kernels: 48.5 us -> 48 us
where the time goes in v6:
time: 48.9 us; the launch traced here: 48.7 us
  Pallas kernels  48 us (98%)
  between operations  0.64 us (1%)
    pallas_call x1, Pallas kernels, per_device(): pl.pallas_call(functools.partial(kernel, ring, band), out_shape=(out, out...  46.5 us
    pallas_call x1, Pallas kernels, per_device(): pl.pallas_call(deliver, out_shape=(out, out), in_specs=[hbm] * 2, out_spe...  1.48 us

profile of v6, /device:TPU:1, one launch (start us, length us, event | category | flops | bytes accessed | tf_op | source)
XLA Modules:
  0.0 48.7 jit_solution(8477687217224487126)
XLA Ops:
  0.6 46.5 %sweep.1 = (f32[6,2,4,256]{3,2,1,0:T(4,128)}, f32[6,2,4,256]{3,2,1,0:T(4,128)}) custom-call(f32[6,2,4,256]{3,2,1,0:T(4,128)} %adj_r.1, f32[6,2,4,256]{3,2,1,0:T(4,128)} %adj_s.1, f32[6,2,4,256]{3,2,1,0:T(4,128)} %diag_r.1, f32[6,2,4,256]{3,2,1,0:T(4,128)} %diag_s.1, bf16[6,6,2,4,256]{4,3,2,1,0:T(4,128)(2,1)} %off_r.1, bf16[6,6,2,4,256]{4,3,2,1,0:T(4,128)(2,1)} %off_s.1, ...), custom_call_target="tpu_custom_call" | custom-call | tf_op jit(solution)/shard_map/sweep/pallas_call | solution.py:524
  47.2 1.5 %deliver.1 = (f32[6,2,4,256]{3,2,1,0:T(4,128)}, f32[6,2,4,256]{3,2,1,0:T(4,128)}) custom-call(f32[6,2,4,256]{3,2,1,0:T(4,128)} %get-tuple-element.4.from_r, f32[6,2,4,256]{3,2,1,0:T(4,128)} %get-tuple-element.5.from_s), custom_call_target="tpu_custom_call" | custom-call | tf_op jit(solution)/shard_map/deliver/pallas_call | solution.py:593

commit v7 on v6

--- a/solution.py
+++ b/solution.py
@@ -277,9 +277,6 @@
         remote(rstate, home.at[u], send_sem.at[6], land_sem.at[6], circ(-u)).start()
         remote(rstate, home.at[HOMES - u], send_sem.at[6], land_sem.at[6], circ(u)).start()
 
-    edges0_s = begin(edges(adj, 0, 1))
-    edges0_r = begin(edges(adj, 0, 0))
-
 
     copies[2].wait()
     copies[3].wait()
@@ -310,6 +307,8 @@
     sent_n[...] = chosen
     near_b[0] = chosen
     fine(sent_n, near_b, -1, 3)
+    edges0_s = begin(edges(adj, 0, 1))
+    edges0_r = begin(edges(adj, 0, 0))
 
     def wrap(t, size):
         t = t + (size & lax.shift_right_arithmetic(t, 31))

time: 48.9 us -> 49.6 us (1.014)
  Pallas kernels: 48 us -> 48.7 us
    pallas_call x1, Pallas kernels: 46.5 us -> 47.2 us  [per_device(): pl.pallas_call(functools.partial(kernel, ring, band), out_shape=(out, out...]
where the time goes in v7:
time: 49.6 us; the launch traced here: 49.4 us
  Pallas kernels  48.7 us (98%)
  between operations  0.64 us (1%)
    pallas_call x1, Pallas kernels, per_device(): pl.pallas_call(functools.partial(kernel, ring, band), out_shape=(out, out...  47.2 us
    pallas_call x1, Pallas kernels, per_device(): pl.pallas_call(deliver, out_shape=(out, out), in_specs=[hbm] * 2, out_spe...  1.48 us

profile of v7, /device:TPU:1, one launch (start us, length us, event | category | flops | bytes accessed | tf_op | source)
XLA Modules:
  0.0 49.4 jit_solution(14481196902927134121)
XLA Ops:
  0.6 47.2 %sweep.1 = (f32[6,2,4,256]{3,2,1,0:T(4,128)}, f32[6,2,4,256]{3,2,1,0:T(4,128)}) custom-call(f32[6,2,4,256]{3,2,1,0:T(4,128)} %adj_r.1, f32[6,2,4,256]{3,2,1,0:T(4,128)} %adj_s.1, f32[6,2,4,256]{3,2,1,0:T(4,128)} %diag_r.1, f32[6,2,4,256]{3,2,1,0:T(4,128)} %diag_s.1, bf16[6,6,2,4,256]{4,3,2,1,0:T(4,128)(2,1)} %off_r.1, bf16[6,6,2,4,256]{4,3,2,1,0:T(4,128)(2,1)} %off_s.1, ...), custom_call_target="tpu_custom_call" | custom-call | tf_op jit(solution)/shard_map/sweep/pallas_call | solution.py:523
  47.9 1.5 %deliver.1 = (f32[6,2,4,256]{3,2,1,0:T(4,128)}, f32[6,2,4,256]{3,2,1,0:T(4,128)}) custom-call(f32[6,2,4,256]{3,2,1,0:T(4,128)} %get-tuple-element.4.from_r, f32[6,2,4,256]{3,2,1,0:T(4,128)} %get-tuple-element.5.from_s), custom_call_target="tpu_custom_call" | custom-call | tf_op jit(solution)/shard_map/deliver/pallas_call | solution.py:592
